TPU v7x, 32 devices: a whole 2x2x4 slice. The times are simulated.
32 devices in a mesh: gx: 4 (over z), gy: 2 (over y), gz: 4 (over x, core).
Axes of the slice: x: 2, y: 2, z: 4, core: 2. Of those that a mesh axis runs over, the one named last changes fastest.
Arguments:
- saved: float32 [3, 27, 32, 16, 512], P(None, None, 'gx', 'gy', 'gz'), may hold values from 0.02 to 0.08
- porosity: float32 [32, 16, 512], P('gx', 'gy', 'gz'), may hold values from 0.05 to 0.6
- fluid: int32 [32, 16, 512], P('gx', 'gy', 'gz'), may hold values 0 or 1
- seed_adjoint: float32 [27, 32, 16, 512], P(None, 'gx', 'gy', 'gz'), may hold values from -6 to 6
Outputs:
- adjoint_first: float32 [27, 32, 16, 512], P(None, 'gx', 'gy', 'gz')
- porosity_grad: float32 [32, 16, 512], P('gx', 'gy', 'gz')
All inputs are finite; a program needn't handle non-finite values. No bound on the sum of `fluid` on one device may be relied on, other than what follows from the above.
Results may differ from a plain program's by a relative error of at most 0.0001.
Values sent between devices are 32-bit elements; how exact they have to be, the bound alone decides.
No kernel may reach another device: no remote copies, remote signals or barrier semaphores. Data moves between devices by JAX's collectives and lax.ppermute only.
A program may use at most 64 MiB of HBM per device.

v0:
```python
import jax
import jax.numpy as jnp
import numpy as np
from jax import lax
from jax.sharding import PartitionSpec as P

STEPS = 3


def shifted(value, axis, by):
    length = lax.axis_size(axis)
    pairs = [(i, i + by) for i in range(length) if 0 <= i + by < length]
    return lax.ppermute(value, axis, pairs)


def lattice():
    vel = np.array(
        [[a, b, c] for a in (-1, 0, 1) for b in (-1, 0, 1) for c in (-1, 0, 1)], dtype=np.int64
    )
    nonzero = np.abs(vel).sum(axis=1)
    table = np.array([8.0 / 27, 2.0 / 27, 1.0 / 54, 1.0 / 216])
    return (vel, table[nonzero])


def collide(pops, porosity, fluid):
    vel, weights = lattice()
    shape = (27, 1, 1, 1)
    vx = jnp.asarray(vel[:, 0].reshape(shape), jnp.float32)
    vy = jnp.asarray(vel[:, 1].reshape(shape), jnp.float32)
    vz = jnp.asarray(vel[:, 2].reshape(shape), jnp.float32)
    wts = jnp.asarray(weights.reshape(shape), jnp.float32)
    solid = jnp.where(fluid == 1, porosity, jnp.ones_like(porosity))
    density = jnp.sum(pops, axis=0)
    ux = jnp.sum(pops * vx, axis=0) / density
    uy = jnp.sum(pops * vy, axis=0) / density
    uz = jnp.sum(pops * vz, axis=0) / density
    cu = vx * ux + vy * uy + vz * uz
    usq = ux * ux + uy * uy + uz * uz
    equil = wts * density * (1.0 + 3.0 * cu + 4.5 * cu * cu - 1.5 * usq)
    relaxed = pops - 1.6 * (pops - equil)
    return (1.0 - solid) * relaxed + solid * pops[::-1]


def edge_planes(field, dim):
    first = jax.lax.slice_in_dim(field, 0, 1, axis=dim)
    last = jax.lax.slice_in_dim(field, field.shape[dim] - 1, field.shape[dim], axis=dim)
    return (first, last)


def move_along(adjoint, dim):
    vel, weights = lattice()
    column = vel[:, dim - 1]
    upward = [k for k in range(27) if int(column[k]) == 1]
    downward = [k for k in range(27) if int(column[k]) == -1]
    going_up = jnp.stack([adjoint[k] for k in upward], axis=0)
    going_down = jnp.stack([adjoint[k] for k in downward], axis=0)
    first, unused_last = edge_planes(going_up, dim)
    unused_first, last = edge_planes(going_down, dim)
    if dim == 1:
        from_upper = shifted(first, "gx", -1)
        from_lower = shifted(last, "gx", 1)
    elif dim == 2:
        from_upper = shifted(first, "gy", -1)
        from_lower = shifted(last, "gy", 1)
    else:
        from_upper = shifted(first, "gz", -1)
        from_lower = shifted(last, "gz", 1)
    length = adjoint.shape[dim]
    moved_up = jnp.concatenate(
        [jax.lax.slice_in_dim(going_up, 1, length, axis=dim), from_upper], axis=dim
    )
    moved_down = jnp.concatenate(
        [from_lower, jax.lax.slice_in_dim(going_down, 0, length - 1, axis=dim)], axis=dim
    )
    pieces = []
    for index in range(27):
        if int(column[index]) == 1:
            pieces.append(moved_up[upward.index(index)])
        elif int(column[index]) == -1:
            pieces.append(moved_down[downward.index(index)])
        else:
            pieces.append(adjoint[index])
    return jnp.stack(pieces, axis=0)


def local(saved, porosity, fluid, seed_adjoint):
    adjoint = seed_adjoint
    grad = jnp.zeros(porosity.shape, jnp.float32)
    for step in range(STEPS - 1, -1, -1):
        pulled = move_along(move_along(move_along(adjoint, 1), 2), 3)
        outputs, backward = jax.vjp(
            lambda pops, poro: collide(pops, poro, fluid), saved[step], porosity
        )
        adjoint, term = backward(pulled)
        grad = grad + term
    return (adjoint, grad)


def solution(mesh):
    return jax.shard_map(
        local,
        mesh=mesh,
        in_specs=(
            P(None, None, "gx", "gy", "gz"),
            P("gx", "gy", "gz"),
            P("gx", "gy", "gz"),
            P(None, "gx", "gy", "gz"),
        ),
        out_specs=(P(None, "gx", "gy", "gz"), P("gx", "gy", "gz")),
        check_vma=False,
    )
```

profile of v0, /device:TPU:1, one launch (start us, length us, event | category | flops | bytes accessed | tf_op | source)
XLA Modules:
  0.0 104.2 jit_solution(17637651341222521599)
XLA Ops:
  2.9 4.6 %collective-permute-start = (f32[9,1,8,128]{3,2,1,0:T(8,128)S(1)}, f32[9,1,8,128]{3,2,1,0:T(8,128)S(1)}, u32[]{:S(2)}, u32[]{:S(2)}) collective-permute-start(f32[9,1,8,128]{3,2,1,0:T(8,128)S(1)} %get-tuple-element.91), channel_id=1, source_target_pairs={{0,8},{8,16},{16,24},{1,9},{9,17},{17,25},{2,10},{10,18},{18,26},{... | collective-permute-start | bytes 110600 | tf_op jit(solution)/shard_map/ppermute | solution.py:13
  9.6 2.0 %multiply_reduce_fusion.16 = (f32[8,8,128]{2,1,0:T(8,128)S(1)}, f32[8,8,128]{2,1,0:T(8,128)S(1)}, f32[8,8,128]{2,1,0:T(8,128)S(1)}, f32[8,8,128]{2,1,0:T(8,128)S...) fusion(f32[27]{0:T(128)} %constant.31, f32[3,27,8,8,128]{4,3,2,1,0:T(8,128)} %param.16, f32[27]{0:T(128)} %constant.33, ...), kind=kLoop, calls=%fused_computation.84 | loop fusion | flops 2605056 | bytes 1966404 | tf_op jit(solution)/shard_map/jvp()/reduce_sum | solution.py:36
  12.1 3.3 %collective-permute-start.2 = (f32[9,8,1,128]{3,2,1,0:T(1,128)S(1)}, f32[9,8,1,128]{3,2,1,0:T(1,128)S(1)}, u32[]{:S(2)}, u32[]{:S(2)}) collective-permute-start(f32[9,8,1,128]{3,2,1,0:T(1,128)S(1)} %pad_maximum_fusion.14), channel_id=1, source_target_pairs={{0,4},{1,5},{2,6},{3,7},{8,12},{9,13},{10,14},{11,15},{16,20},{17,... | collective-permute-start | bytes 110600 | tf_op jit(solution)/shard_map/ppermute | solution.py:13
  15.5 1.3 %collective-permute-start.3 = (f32[9,8,1,128]{3,2,1,0:T(1,128)S(1)}, f32[9,8,1,128]{3,2,1,0:T(1,128)S(1)}, u32[]{:S(2)}, u32[]{:S(2)}) collective-permute-start(f32[9,8,1,128]{3,2,1,0:T(1,128)S(1)} %pad_maximum_fusion.13), channel_id=1, source_target_pairs={{4,0},{5,1},{6,2},{7,3},{12,8},{13,9},{14,10},{15,11},{20,16},{21,... | collective-permute-start | bytes 110600 | tf_op jit(solution)/shard_map/ppermute | solution.py:13
  16.9 3.3 %collective-permute-done.3 = f32[9,8,1,128]{3,2,1,0:T(1,128)S(1)} collective-permute-done((f32[9,8,1,128]{3,2,1,0:T(1,128)S(1)}, f32[9,8,1,128]{3,2,1,0:T(1,128)S(1)}, u32[]{:S(2)}, u32[]{:S(2)}) %collective-permute-start.3) | collective-permute-done | bytes 36896 | tf_op jit(solution)/shard_map/ppermute | solution.py:13
  21.3 5.7 %collective-permute-start.4 = (f32[9,8,8,1]{3,2,1,0:T(8,128)S(1)}, f32[9,8,8,1]{3,2,1,0:T(8,128)S(1)}, u32[]{:S(2)}, u32[]{:S(2)}) collective-permute-start(f32[9,8,8,1]{3,2,1,0:T(8,128)S(1)} %slice.916), channel_id=1, source_target_pairs={{0,1},{1,2},{2,3},{4,5},{5,6},{6,7},{8,9},{9,10},{10,11},{12,13},{... | collective-permute-start | bytes 6920 | tf_op jit(solution)/shard_map/ppermute | solution.py:13
  27.2 1.9 %collective-permute-start.5 = (f32[9,8,8,1]{3,2,1,0:T(8,128)S(1)}, f32[9,8,8,1]{3,2,1,0:T(8,128)S(1)}, u32[]{:S(2)}, u32[]{:S(2)}) collective-permute-start(f32[9,8,8,1]{3,2,1,0:T(8,128)S(1)} %bitcast.63), channel_id=1, source_target_pairs={{1,0},{2,1},{3,2},{5,4},{6,5},{7,6},{9,8},{10,9},{11,10},{13,12},{... | collective-permute-start | bytes 6920 | tf_op jit(solution)/shard_map/ppermute | solution.py:13
  29.1 1.5 %collective-permute-done.4 = f32[9,8,8,1]{3,2,1,0:T(8,128)S(1)} collective-permute-done((f32[9,8,8,1]{3,2,1,0:T(8,128)S(1)}, f32[9,8,8,1]{3,2,1,0:T(8,128)S(1)}, u32[]{:S(2)}, u32[]{:S(2)}) %collective-permute-start.4) | collective-permute-done | bytes 2336 | tf_op jit(solution)/shard_map/ppermute | solution.py:13
  30.7 4.5 %collective-permute-done.5 = f32[9,8,8,1]{3,2,1,0:T(8,128)S(1)} collective-permute-done((f32[9,8,8,1]{3,2,1,0:T(8,128)S(1)}, f32[9,8,8,1]{3,2,1,0:T(8,128)S(1)}, u32[]{:S(2)}, u32[]{:S(2)}) %collective-permute-start.5) | collective-permute-done | bytes 2336 | tf_op jit(solution)/shard_map/ppermute | solution.py:13
  37.5 1.5 %fusion.27 = (f32[8,8,128]{2,1,0:T(8,128)S(1)}, f32[8,8,128]{2,1,0:T(8,128)S(1)}, f32[8,8,128]{2,1,0:T(8,128)S(1)}, f32[8,8,128]{2,1,0:T(8,128)S(1)}, f32[8,8,12...) fusion(f32[27,8,8,128]{3,2,1,0:T(8,128)S(1)} %constant_dynamic-update-slice_fusion.18, ...), kind=kLoop, calls=%fused_computation.126 | loop fusion | flops 7913472 | bytes 3080624 | tf_op jit(solution)/shard_map/transpose(jvp())/reduce_sum | solution.py:39
  39.5 3.2 %collective-permute-start.6 = (f32[9,1,8,128]{3,2,1,0:T(8,128)S(1)}, f32[9,1,8,128]{3,2,1,0:T(8,128)S(1)}, u32[]{:S(2)}, u32[]{:S(2)}) collective-permute-start(f32[9,1,8,128]{3,2,1,0:T(8,128)S(1)} %get-tuple-element.82), channel_id=1, source_target_pairs={{0,8},{8,16},{16,24},{1,9},{9,17},{17,25},{2,10},{10,18},{18,26},{... | collective-permute-start | bytes 110600 | tf_op jit(solution)/shard_map/ppermute | solution.py:13
  42.7 1.3 %collective-permute-start.7 = (f32[9,1,8,128]{3,2,1,0:T(8,128)S(1)}, f32[9,1,8,128]{3,2,1,0:T(8,128)S(1)}, u32[]{:S(2)}, u32[]{:S(2)}) collective-permute-start(f32[9,1,8,128]{3,2,1,0:T(8,128)S(1)} %get-tuple-element.83), channel_id=1, source_target_pairs={{8,0},{16,8},{24,16},{9,1},{17,9},{25,17},{10,2},{18,10},{26,18},{... | collective-permute-start | bytes 110600 | tf_op jit(solution)/shard_map/ppermute | solution.py:13
  44.1 3.4 %collective-permute-done.7 = f32[9,1,8,128]{3,2,1,0:T(8,128)S(1)} collective-permute-done((f32[9,1,8,128]{3,2,1,0:T(8,128)S(1)}, f32[9,1,8,128]{3,2,1,0:T(8,128)S(1)}, u32[]{:S(2)}, u32[]{:S(2)}) %collective-permute-start.7) | collective-permute-done | bytes 36896 | tf_op jit(solution)/shard_map/ppermute | solution.py:13
  47.5 1.3 %collective-permute-start.8 = (f32[9,8,1,128]{3,2,1,0:T(1,128)S(1)}, f32[9,8,1,128]{3,2,1,0:T(1,128)S(1)}, u32[]{:S(2)}, u32[]{:S(2)}) collective-permute-start(f32[9,8,1,128]{3,2,1,0:T(1,128)S(1)} %pad_maximum_fusion.12), channel_id=1, source_target_pairs={{0,4},{1,5},{2,6},{3,7},{8,12},{9,13},{10,14},{11,15},{16,20},{17,... | collective-permute-start | bytes 110600 | tf_op jit(solution)/shard_map/ppermute | solution.py:13
  48.9 1.3 %collective-permute-start.9 = (f32[9,8,1,128]{3,2,1,0:T(1,128)S(1)}, f32[9,8,1,128]{3,2,1,0:T(1,128)S(1)}, u32[]{:S(2)}, u32[]{:S(2)}) collective-permute-start(f32[9,8,1,128]{3,2,1,0:T(1,128)S(1)} %pad_maximum_fusion.11), channel_id=1, source_target_pairs={{4,0},{5,1},{6,2},{7,3},{12,8},{13,9},{14,10},{15,11},{20,16},{21,... | collective-permute-start | bytes 110600 | tf_op jit(solution)/shard_map/ppermute | solution.py:13
  50.3 3.3 %collective-permute-done.9 = f32[9,8,1,128]{3,2,1,0:T(1,128)S(1)} collective-permute-done((f32[9,8,1,128]{3,2,1,0:T(1,128)S(1)}, f32[9,8,1,128]{3,2,1,0:T(1,128)S(1)}, u32[]{:S(2)}, u32[]{:S(2)}) %collective-permute-start.9) | collective-permute-done | bytes 36896 | tf_op jit(solution)/shard_map/ppermute | solution.py:13
  53.9 4.6 %collective-permute-start.10 = (f32[9,8,8,1]{3,2,1,0:T(8,128)S(1)}, f32[9,8,8,1]{3,2,1,0:T(8,128)S(1)}, u32[]{:S(2)}, u32[]{:S(2)}) collective-permute-start(f32[9,8,8,1]{3,2,1,0:T(8,128)S(1)} %slice.1001), channel_id=1, source_target_pairs={{0,1},{1,2},{2,3},{4,5},{5,6},{6,7},{8,9},{9,10},{10,11},{12,13},{... | collective-permute-start | bytes 6920 | tf_op jit(solution)/shard_map/ppermute | solution.py:13
  58.7 1.9 %collective-permute-start.11 = (f32[9,8,8,1]{3,2,1,0:T(8,128)S(1)}, f32[9,8,8,1]{3,2,1,0:T(8,128)S(1)}, u32[]{:S(2)}, u32[]{:S(2)}) collective-permute-start(f32[9,8,8,1]{3,2,1,0:T(8,128)S(1)} %bitcast.64), channel_id=1, source_target_pairs={{1,0},{2,1},{3,2},{5,4},{6,5},{7,6},{9,8},{10,9},{11,10},{13,12},{... | collective-permute-start | bytes 6920 | tf_op jit(solution)/shard_map/ppermute | solution.py:13
  60.6 1.5 %collective-permute-done.10 = f32[9,8,8,1]{3,2,1,0:T(8,128)S(1)} collective-permute-done((f32[9,8,8,1]{3,2,1,0:T(8,128)S(1)}, f32[9,8,8,1]{3,2,1,0:T(8,128)S(1)}, u32[]{:S(2)}, u32[]{:S(2)}) %collective-permute-start.10) | collective-permute-done | bytes 2336 | tf_op jit(solution)/shard_map/ppermute | solution.py:13
  62.2 4.5 %collective-permute-done.11 = f32[9,8,8,1]{3,2,1,0:T(8,128)S(1)} collective-permute-done((f32[9,8,8,1]{3,2,1,0:T(8,128)S(1)}, f32[9,8,8,1]{3,2,1,0:T(8,128)S(1)}, u32[]{:S(2)}, u32[]{:S(2)}) %collective-permute-start.11) | collective-permute-done | bytes 2336 | tf_op jit(solution)/shard_map/ppermute | solution.py:13
  68.2 1.9 %multiply_reduce_fusion.11 = (f32[8,8,128]{2,1,0:T(8,128)S(1)}, f32[8,8,128]{2,1,0:T(8,128)S(1)}, f32[8,8,128]{2,1,0:T(8,128)S(1)}, f32[8,8,128]{2,1,0:T(8,128)S...) fusion(f32[27]{0:T(128)S(1)} %copy-done.4, ...), kind=kLoop, calls=%fused_computation.78 | loop fusion | flops 10534912 | bytes 4981168 | tf_op jit(solution)/shard_map/transpose(jvp())/reduce_sum | solution.py:37
  70.6 3.2 %collective-permute-start.12 = (f32[9,1,8,128]{3,2,1,0:T(8,128)S(1)}, f32[9,1,8,128]{3,2,1,0:T(8,128)S(1)}, u32[]{:S(2)}, u32[]{:S(2)}) collective-permute-start(f32[9,1,8,128]{3,2,1,0:T(8,128)S(1)} %get-tuple-element.73), channel_id=1, source_target_pairs={{0,8},{8,16},{16,24},{1,9},{9,17},{17,25},{2,10},{10,18},{18,26},{... | collective-permute-start | bytes 110600 | tf_op jit(solution)/shard_map/ppermute | solution.py:13
  75.2 3.4 %collective-permute-done.13 = f32[9,1,8,128]{3,2,1,0:T(8,128)S(1)} collective-permute-done((f32[9,1,8,128]{3,2,1,0:T(8,128)S(1)}, f32[9,1,8,128]{3,2,1,0:T(8,128)S(1)}, u32[]{:S(2)}, u32[]{:S(2)}) %collective-permute-start.13) | collective-permute-done | bytes 36896 | tf_op jit(solution)/shard_map/ppermute | solution.py:13
  78.6 1.3 %collective-permute-start.14 = (f32[9,8,1,128]{3,2,1,0:T(1,128)S(1)}, f32[9,8,1,128]{3,2,1,0:T(1,128)S(1)}, u32[]{:S(2)}, u32[]{:S(2)}) collective-permute-start(f32[9,8,1,128]{3,2,1,0:T(1,128)S(1)} %pad_maximum_fusion.10), channel_id=1, source_target_pairs={{0,4},{1,5},{2,6},{3,7},{8,12},{9,13},{10,14},{11,15},{16,20},{17,... | collective-permute-start | bytes 110600 | tf_op jit(solution)/shard_map/ppermute | solution.py:13
  80.0 1.3 %collective-permute-start.15 = (f32[9,8,1,128]{3,2,1,0:T(1,128)S(1)}, f32[9,8,1,128]{3,2,1,0:T(1,128)S(1)}, u32[]{:S(2)}, u32[]{:S(2)}) collective-permute-start(f32[9,8,1,128]{3,2,1,0:T(1,128)S(1)} %pad_maximum_fusion.9), channel_id=1, source_target_pairs={{4,0},{5,1},{6,2},{7,3},{12,8},{13,9},{14,10},{15,11},{20,16},{21,... | collective-permute-start | bytes 110600 | tf_op jit(solution)/shard_map/ppermute | solution.py:13
  81.4 3.3 %collective-permute-done.15 = f32[9,8,1,128]{3,2,1,0:T(1,128)S(1)} collective-permute-done((f32[9,8,1,128]{3,2,1,0:T(1,128)S(1)}, f32[9,8,1,128]{3,2,1,0:T(1,128)S(1)}, u32[]{:S(2)}, u32[]{:S(2)}) %collective-permute-start.15) | collective-permute-done | bytes 36896 | tf_op jit(solution)/shard_map/ppermute | solution.py:13
  85.0 4.6 %collective-permute-start.16 = (f32[9,8,8,1]{3,2,1,0:T(8,128)S(1)}, f32[9,8,8,1]{3,2,1,0:T(8,128)S(1)}, u32[]{:S(2)}, u32[]{:S(2)}) collective-permute-start(f32[9,8,8,1]{3,2,1,0:T(8,128)S(1)} %slice.1088), channel_id=1, source_target_pairs={{0,1},{1,2},{2,3},{4,5},{5,6},{6,7},{8,9},{9,10},{10,11},{12,13},{... | collective-permute-start | bytes 6920 | tf_op jit(solution)/shard_map/ppermute | solution.py:13
  89.8 2.1 %collective-permute-start.17 = (f32[9,8,8,1]{3,2,1,0:T(8,128)S(1)}, f32[9,8,8,1]{3,2,1,0:T(8,128)S(1)}, u32[]{:S(2)}, u32[]{:S(2)}) collective-permute-start(f32[9,8,8,1]{3,2,1,0:T(8,128)S(1)} %bitcast.65), channel_id=1, source_target_pairs={{1,0},{2,1},{3,2},{5,4},{6,5},{7,6},{9,8},{10,9},{11,10},{13,12},{... | collective-permute-start | bytes 6920 | tf_op jit(solution)/shard_map/ppermute | solution.py:13
  91.9 1.4 %collective-permute-done.16 = f32[9,8,8,1]{3,2,1,0:T(8,128)S(1)} collective-permute-done((f32[9,8,8,1]{3,2,1,0:T(8,128)S(1)}, f32[9,8,8,1]{3,2,1,0:T(8,128)S(1)}, u32[]{:S(2)}, u32[]{:S(2)}) %collective-permute-start.16) | collective-permute-done | bytes 2336 | tf_op jit(solution)/shard_map/ppermute | solution.py:13
  93.4 4.5 %collective-permute-done.17 = f32[9,8,8,1]{3,2,1,0:T(8,128)S(1)} collective-permute-done((f32[9,8,8,1]{3,2,1,0:T(8,128)S(1)}, f32[9,8,8,1]{3,2,1,0:T(8,128)S(1)}, u32[]{:S(2)}, u32[]{:S(2)}) %collective-permute-start.17) | collective-permute-done | bytes 2336 | tf_op jit(solution)/shard_map/ppermute | solution.py:13
  99.4 2.5 %fusion.4 = (f32[8,8,128]{2,1,0:T(8,128)S(1)}, f32[8,8,128]{2,1,0:T(8,128)S(1)}, f32[8,8,128]{2,1,0:T(8,128)S(1)}, f32[8,8,128]{2,1,0:T(8,128)S(1)}, f32[27,8,8,128]{3,2,1,0:T(8,128)S(1)}) fusion(f32[27,8,8,128]{3,2,1,0:T(8,128)S(1)} %constant_dynamic-update-slice_fusion.18, f32[8,8,128]{2,1,0:T(8,128)S(1)} %get-tuple-element.56, ...), kind=kLoop, calls=%fused_computation.40 | loop fusion | flops 11247616 | bytes 4915632 | tf_op jit(solution)/shard_map/transpose(jvp())/reduce_sum | solution.py:41
  102.2 1.4 %multiply_reduce_fusion = (f32[8,8,128]{2,1,0:T(8,128)S(1)}, f32[27,8,8,128]{3,2,1,0:T(8,128)}) fusion(f32[27,8,8,128]{3,2,1,0:T(8,128)S(1)} %constant_dynamic-update-slice_fusion.108, f32[27,8,8,128]{3,2,1,0:T(8,128)S(1)} %get-tuple-element.63, f32[8,8,128]{2,1,0:T(8,128)S(1)} %get-tuple-element.138, f32[27]{0:T(128)S(1)} %copy-done.4, ...), kind=kLoop, calls=%fused_computation.63 | loop fusion | flops 3088384 | bytes 3735876 | tf_op jit(solution)/shard_map/transpose(jvp())/reduce_sum | solution.py:41
  (188 shorter events, 15.8 us)
Async XLA Ops:
  0.6 11.0 %copy-start = (f32[3,27,8,8,128]{4,3,2,1,0:T(8,128)S(1)}, f32[3,27,8,8,128]{4,3,2,1,0:T(8,128)}, u32[]{:S(2)}) copy-start(f32[3,27,8,8,128]{4,3,2,1,0:T(8,128)} %param.16) | copy-start | bytes 7962628
  1.6 10.4 %collective-permute-start.1 = (f32[9,1,8,128]{3,2,1,0:T(8,128)S(1)}, f32[9,1,8,128]{3,2,1,0:T(8,128)S(1)}, u32[]{:S(2)}, u32[]{:S(2)}) collective-permute-start(f32[9,1,8,128]{3,2,1,0:T(8,128)S(1)} %get-tuple-element.92), channel_id=1, source_target_pairs={{8,0},{16,8},{24,16},{9,1},{17,9},{25,17},{10,2},{18,10},{26,18},{... | collective-permute-start | bytes 110600 | tf_op jit(solution)/shard_map/ppermute | solution.py:13
  2.9 9.1 %collective-permute-start = (f32[9,1,8,128]{3,2,1,0:T(8,128)S(1)}, f32[9,1,8,128]{3,2,1,0:T(8,128)S(1)}, u32[]{:S(2)}, u32[]{:S(2)}) collective-permute-start(f32[9,1,8,128]{3,2,1,0:T(8,128)S(1)} %get-tuple-element.91), channel_id=1, source_target_pairs={{0,8},{8,16},{16,24},{1,9},{9,17},{17,25},{2,10},{10,18},{18,26},{... | collective-permute-start | bytes 110600 | tf_op jit(solution)/shard_map/ppermute | solution.py:13
  12.1 4.7 %collective-permute-start.2 = (f32[9,8,1,128]{3,2,1,0:T(1,128)S(1)}, f32[9,8,1,128]{3,2,1,0:T(1,128)S(1)}, u32[]{:S(2)}, u32[]{:S(2)}) collective-permute-start(f32[9,8,1,128]{3,2,1,0:T(1,128)S(1)} %pad_maximum_fusion.14), channel_id=1, source_target_pairs={{0,4},{1,5},{2,6},{3,7},{8,12},{9,13},{10,14},{11,15},{16,20},{17,... | collective-permute-start | bytes 110600 | tf_op jit(solution)/shard_map/ppermute | solution.py:13
  15.4 11.5 %copy-start.1 = (f32[8,8,128]{2,1,0:T(8,128)S(1)}, f32[8,8,128]{2,1,0:T(8,128)}, u32[]{:S(2)}) copy-start(f32[8,8,128]{2,1,0:T(8,128)} %param.17) | copy-start | bytes 98308
  15.4 11.5 %copy-start.2 = (s32[8,8,128]{2,1,0:T(8,128)S(1)}, s32[8,8,128]{2,1,0:T(8,128)}, u32[]{:S(2)}) copy-start(s32[8,8,128]{2,1,0:T(8,128)} %param.18) | copy-start | bytes 98308
  15.5 4.7 %collective-permute-start.3 = (f32[9,8,1,128]{3,2,1,0:T(1,128)S(1)}, f32[9,8,1,128]{3,2,1,0:T(1,128)S(1)}, u32[]{:S(2)}, u32[]{:S(2)}) collective-permute-start(f32[9,8,1,128]{3,2,1,0:T(1,128)S(1)} %pad_maximum_fusion.13), channel_id=1, source_target_pairs={{4,0},{5,1},{6,2},{7,3},{12,8},{13,9},{14,10},{15,11},{20,16},{21,... | collective-permute-start | bytes 110600 | tf_op jit(solution)/shard_map/ppermute | solution.py:13
  21.3 9.3 %collective-permute-start.4 = (f32[9,8,8,1]{3,2,1,0:T(8,128)S(1)}, f32[9,8,8,1]{3,2,1,0:T(8,128)S(1)}, u32[]{:S(2)}, u32[]{:S(2)}) collective-permute-start(f32[9,8,8,1]{3,2,1,0:T(8,128)S(1)} %slice.916), channel_id=1, source_target_pairs={{0,1},{1,2},{2,3},{4,5},{5,6},{6,7},{8,9},{9,10},{10,11},{12,13},{... | collective-permute-start | bytes 6920 | tf_op jit(solution)/shard_map/ppermute | solution.py:13
  27.2 8.0 %collective-permute-start.5 = (f32[9,8,8,1]{3,2,1,0:T(8,128)S(1)}, f32[9,8,8,1]{3,2,1,0:T(8,128)S(1)}, u32[]{:S(2)}, u32[]{:S(2)}) collective-permute-start(f32[9,8,8,1]{3,2,1,0:T(8,128)S(1)} %bitcast.63), channel_id=1, source_target_pairs={{1,0},{2,1},{3,2},{5,4},{6,5},{7,6},{9,8},{10,9},{11,10},{13,12},{... | collective-permute-start | bytes 6920 | tf_op jit(solution)/shard_map/ppermute | solution.py:13
  36.8 0.7 copy-start.3
  36.8 0.7 copy-start.4
  36.8 0.7 copy-start.5
  36.9 0.7 copy-start.6
  39.5 4.5 %collective-permute-start.6 = (f32[9,1,8,128]{3,2,1,0:T(8,128)S(1)}, f32[9,1,8,128]{3,2,1,0:T(8,128)S(1)}, u32[]{:S(2)}, u32[]{:S(2)}) collective-permute-start(f32[9,1,8,128]{3,2,1,0:T(8,128)S(1)} %get-tuple-element.82), channel_id=1, source_target_pairs={{0,8},{8,16},{16,24},{1,9},{9,17},{17,25},{2,10},{10,18},{18,26},{... | collective-permute-start | bytes 110600 | tf_op jit(solution)/shard_map/ppermute | solution.py:13
  42.7 4.7 %collective-permute-start.7 = (f32[9,1,8,128]{3,2,1,0:T(8,128)S(1)}, f32[9,1,8,128]{3,2,1,0:T(8,128)S(1)}, u32[]{:S(2)}, u32[]{:S(2)}) collective-permute-start(f32[9,1,8,128]{3,2,1,0:T(8,128)S(1)} %get-tuple-element.83), channel_id=1, source_target_pairs={{8,0},{16,8},{24,16},{9,1},{17,9},{25,17},{10,2},{18,10},{26,18},{... | collective-permute-start | bytes 110600 | tf_op jit(solution)/shard_map/ppermute | solution.py:13
  47.5 2.7 %collective-permute-start.8 = (f32[9,8,1,128]{3,2,1,0:T(1,128)S(1)}, f32[9,8,1,128]{3,2,1,0:T(1,128)S(1)}, u32[]{:S(2)}, u32[]{:S(2)}) collective-permute-start(f32[9,8,1,128]{3,2,1,0:T(1,128)S(1)} %pad_maximum_fusion.12), channel_id=1, source_target_pairs={{0,4},{1,5},{2,6},{3,7},{8,12},{9,13},{10,14},{11,15},{16,20},{17,... | collective-permute-start | bytes 110600 | tf_op jit(solution)/shard_map/ppermute | solution.py:13
  48.9 4.7 %collective-permute-start.9 = (f32[9,8,1,128]{3,2,1,0:T(1,128)S(1)}, f32[9,8,1,128]{3,2,1,0:T(1,128)S(1)}, u32[]{:S(2)}, u32[]{:S(2)}) collective-permute-start(f32[9,8,1,128]{3,2,1,0:T(1,128)S(1)} %pad_maximum_fusion.11), channel_id=1, source_target_pairs={{4,0},{5,1},{6,2},{7,3},{12,8},{13,9},{14,10},{15,11},{20,16},{21,... | collective-permute-start | bytes 110600 | tf_op jit(solution)/shard_map/ppermute | solution.py:13
  53.9 8.3 %collective-permute-start.10 = (f32[9,8,8,1]{3,2,1,0:T(8,128)S(1)}, f32[9,8,8,1]{3,2,1,0:T(8,128)S(1)}, u32[]{:S(2)}, u32[]{:S(2)}) collective-permute-start(f32[9,8,8,1]{3,2,1,0:T(8,128)S(1)} %slice.1001), channel_id=1, source_target_pairs={{0,1},{1,2},{2,3},{4,5},{5,6},{6,7},{8,9},{9,10},{10,11},{12,13},{... | collective-permute-start | bytes 6920 | tf_op jit(solution)/shard_map/ppermute | solution.py:13
  58.7 8.0 %collective-permute-start.11 = (f32[9,8,8,1]{3,2,1,0:T(8,128)S(1)}, f32[9,8,8,1]{3,2,1,0:T(8,128)S(1)}, u32[]{:S(2)}, u32[]{:S(2)}) collective-permute-start(f32[9,8,8,1]{3,2,1,0:T(8,128)S(1)} %bitcast.64), channel_id=1, source_target_pairs={{1,0},{2,1},{3,2},{5,4},{6,5},{7,6},{9,8},{10,9},{11,10},{13,12},{... | collective-permute-start | bytes 6920 | tf_op jit(solution)/shard_map/ppermute | solution.py:13
  70.6 4.5 %collective-permute-start.12 = (f32[9,1,8,128]{3,2,1,0:T(8,128)S(1)}, f32[9,1,8,128]{3,2,1,0:T(8,128)S(1)}, u32[]{:S(2)}, u32[]{:S(2)}) collective-permute-start(f32[9,1,8,128]{3,2,1,0:T(8,128)S(1)} %get-tuple-element.73), channel_id=1, source_target_pairs={{0,8},{8,16},{16,24},{1,9},{9,17},{17,25},{2,10},{10,18},{18,26},{... | collective-permute-start | bytes 110600 | tf_op jit(solution)/shard_map/ppermute | solution.py:13
  73.8 4.7 %collective-permute-start.13 = (f32[9,1,8,128]{3,2,1,0:T(8,128)S(1)}, f32[9,1,8,128]{3,2,1,0:T(8,128)S(1)}, u32[]{:S(2)}, u32[]{:S(2)}) collective-permute-start(f32[9,1,8,128]{3,2,1,0:T(8,128)S(1)} %get-tuple-element.74), channel_id=1, source_target_pairs={{8,0},{16,8},{24,16},{9,1},{17,9},{25,17},{10,2},{18,10},{26,18},{... | collective-permute-start | bytes 110600 | tf_op jit(solution)/shard_map/ppermute | solution.py:13
  78.6 2.7 %collective-permute-start.14 = (f32[9,8,1,128]{3,2,1,0:T(1,128)S(1)}, f32[9,8,1,128]{3,2,1,0:T(1,128)S(1)}, u32[]{:S(2)}, u32[]{:S(2)}) collective-permute-start(f32[9,8,1,128]{3,2,1,0:T(1,128)S(1)} %pad_maximum_fusion.10), channel_id=1, source_target_pairs={{0,4},{1,5},{2,6},{3,7},{8,12},{9,13},{10,14},{11,15},{16,20},{17,... | collective-permute-start | bytes 110600 | tf_op jit(solution)/shard_map/ppermute | solution.py:13
  80.0 4.7 %collective-permute-start.15 = (f32[9,8,1,128]{3,2,1,0:T(1,128)S(1)}, f32[9,8,1,128]{3,2,1,0:T(1,128)S(1)}, u32[]{:S(2)}, u32[]{:S(2)}) collective-permute-start(f32[9,8,1,128]{3,2,1,0:T(1,128)S(1)} %pad_maximum_fusion.9), channel_id=1, source_target_pairs={{4,0},{5,1},{6,2},{7,3},{12,8},{13,9},{14,10},{15,11},{20,16},{21,... | collective-permute-start | bytes 110600 | tf_op jit(solution)/shard_map/ppermute | solution.py:13
  85.0 8.3 %collective-permute-start.16 = (f32[9,8,8,1]{3,2,1,0:T(8,128)S(1)}, f32[9,8,8,1]{3,2,1,0:T(8,128)S(1)}, u32[]{:S(2)}, u32[]{:S(2)}) collective-permute-start(f32[9,8,8,1]{3,2,1,0:T(8,128)S(1)} %slice.1088), channel_id=1, source_target_pairs={{0,1},{1,2},{2,3},{4,5},{5,6},{6,7},{8,9},{9,10},{10,11},{12,13},{... | collective-permute-start | bytes 6920 | tf_op jit(solution)/shard_map/ppermute | solution.py:13
  89.8 8.0 %collective-permute-start.17 = (f32[9,8,8,1]{3,2,1,0:T(8,128)S(1)}, f32[9,8,8,1]{3,2,1,0:T(8,128)S(1)}, u32[]{:S(2)}, u32[]{:S(2)}) collective-permute-start(f32[9,8,8,1]{3,2,1,0:T(8,128)S(1)} %bitcast.65), channel_id=1, source_target_pairs={{1,0},{2,1},{3,2},{5,4},{6,5},{7,6},{9,8},{10,9},{11,10},{13,12},{... | collective-permute-start | bytes 6920 | tf_op jit(solution)/shard_map/ppermute | solution.py:13
where the time goes:
time: 105 us; the launch traced here: 104 us
  starting transfers between devices  45.6 us (43%)
  waiting for transfers between devices  34.5 us (33%)
  other arithmetic  16.6 us (16%)
  local copies, waits for them, and re-layouts  5.81 us (6%)
  between operations  1.72 us (2%)
    ppermute x18, starting transfers between devices, shifted(): return lax.ppermute(value, axis, pairs)  45.6 us
    ppermute x18, waiting for transfers between devices, shifted(): return lax.ppermute(value, axis, pairs)  34.5 us
    unnamed x81, other arithmetic  4.24 us
    reduce_sum x2, other arithmetic, collide(): return (1.0 - solid) * relaxed + solid * pops[::-1]  3.87 us
    reduce_sum x2, other arithmetic, collide(): cu = vx * ux + vy * uy + vz * uz  2.16 us
  transfers between devices with their start and end apart: 18, of which 11 were waited for; matrix products, arithmetic and copies ran while one was open for 5% of the time, Pallas kernels for 0%

commit v1 on v0

--- a/solution.py
+++ b/solution.py
@@ -7,10 +7,33 @@
 STEPS = 3
 
 
-def shifted(value, axis, by):
+def swapped(value, axis, odd, spare):
     length = lax.axis_size(axis)
-    pairs = [(i, i + by) for i in range(length) if 0 <= i + by < length]
-    return lax.ppermute(value, axis, pairs)
+    wide = lax.axis_size(spare) if spare else 1
+    pairs = []
+    for i in range(length):
+        for k in range(wide):
+            j, m = ((i + 1 if i % 2 == 1 else i - 1) if odd else i ^ 1), k
+            if not 0 <= j < length:
+                j, m = (i, k ^ 1) if spare else (j % length, k)
+            if j < length and m < wide:
+                pairs.append((i * wide + k, j * wide + m))
+    return lax.ppermute(value, (axis, spare) if spare else axis, pairs)
+
+
+def exchanged(to_lower, to_upper, axis, spare):
+    length = lax.axis_size(axis)
+    index = lax.axis_index(axis)
+    even = index % 2 == 0
+    first = swapped(jnp.where(even, to_upper, to_lower), axis, False, spare)
+    if length > 2:
+        second = swapped(jnp.where(even, to_lower, to_upper), axis, True, spare)
+    else:
+        second = jnp.zeros_like(first)
+    zero = jnp.zeros_like(first)
+    from_upper = jnp.where(index == length - 1, zero, jnp.where(even, first, second))
+    from_lower = jnp.where(index == 0, zero, jnp.where(even, second, first))
+    return (from_upper, from_lower)
 
 
 def lattice():
@@ -56,15 +79,8 @@
     going_down = jnp.stack([adjoint[k] for k in downward], axis=0)
     first, unused_last = edge_planes(going_up, dim)
     unused_first, last = edge_planes(going_down, dim)
-    if dim == 1:
-        from_upper = shifted(first, "gx", -1)
-        from_lower = shifted(last, "gx", 1)
-    elif dim == 2:
-        from_upper = shifted(first, "gy", -1)
-        from_lower = shifted(last, "gy", 1)
-    else:
-        from_upper = shifted(first, "gz", -1)
-        from_lower = shifted(last, "gz", 1)
+    axis, spare = {1: ("gx", "gz"), 2: ("gy", "gz"), 3: ("gz", None)}[dim]
+    from_upper, from_lower = exchanged(first, last, axis, spare)
     length = adjoint.shape[dim]
     moved_up = jnp.concatenate(
         [jax.lax.slice_in_dim(going_up, 1, length, axis=dim), from_upper], axis=dim

time: 105 us -> 91.7 us (0.87)
  the two profiles are of different devices: /device:TPU:1 before, /device:TPU:0 now
where the time goes in v1:
time: 91.7 us; the launch traced here: 90.6 us
  other arithmetic  30.3 us (33%)
  waiting for transfers between devices  30.2 us (33%)
  starting transfers between devices  17.3 us (19%)
  local copies, waits for them, and re-layouts  11.3 us (12%)
  between operations  1.61 us (2%)
    ppermute x15, waiting for transfers between devices, swapped(): return lax.ppermute(value, (axis, spare) if spare else axis, pairs)  30.2 us
    ppermute x15, starting transfers between devices, swapped(): return lax.ppermute(value, (axis, spare) if spare else axis, pairs)  17.3 us
    unnamed x99, local copies, waits for them, and re-layouts  7.72 us
    unnamed x63, other arithmetic  5.42 us
    reduce_sum x2, other arithmetic, collide(): return (1.0 - solid) * relaxed + solid * pops[::-1]  3.82 us
    select_n x6, other arithmetic, exchanged(): first = swapped(jnp.where(even, to_upper, to_lower), axis, False, spare)  2.95 us
    reduce_sum x1, other arithmetic, collide(): uz = jnp.sum(pops * vz, axis=0) / density  2.65 us
    reduce_sum x1, other arithmetic, collide(): density = jnp.sum(pops, axis=0)  2.23 us
  transfers between devices with their start and end apart: 15, of which 8 were waited for; matrix products, arithmetic and copies ran while one was open for 11% of the time, Pallas kernels for 0%

profile of v1, /device:TPU:0, one launch (start us, length us, event | category | flops | bytes accessed | tf_op | source)
XLA Modules:
  0.0 90.6 jit_solution(7894830532519401108)
XLA Ops:
  0.7 0.9 %slice_select_fusion.11 = (f32[9,1,8,128]{3,2,1,0:T(8,128)S(1)}, f32[9,1,8,128]{3,2,1,0:T(8,128)S(1)}) fusion(f32[27,8,8,128]{3,2,1,0:T(8,128)} %param.19, pred[]{:T(512)S(6)} %eq.66), kind=kLoop, calls=%fused_computation.431 | loop fusion | flops 18432 | bytes 147457 | tf_op jit(solution)/shard_map/jit(_where)/select_n | solution.py:30
  2.1 4.1 %collective-permute-start.1 = (f32[9,1,8,128]{3,2,1,0:T(8,128)S(1)}, f32[9,1,8,128]{3,2,1,0:T(8,128)S(1)}, u32[]{:S(2)}, u32[]{:S(2)}) collective-permute-start(f32[9,1,8,128]{3,2,1,0:T(8,128)S(1)} %get-tuple-element.94), channel_id=1, source_target_pairs={{0,8},{1,9},{2,10},{3,11},{8,0},{9,1},{10,2},{11,3},{16,24},{17,25... | collective-permute-start | bytes 110600 | tf_op jit(solution)/shard_map/ppermute | solution.py:21
  6.2 1.1 %fusion.122 = (f32[9,7,8,128]{3,2,1,0:T(8,128)S(1)}, f32[9,7,8,128]{3,2,1,0:T(8,128)S(1)}) fusion(f32[27,8,8,128]{3,2,1,0:T(8,128)} %param.19), kind=kLoop, calls=%fused_computation.540 | loop fusion | bytes 1032192 | tf_op jit(solution)/shard_map/slice | solution.py:89
  7.3 1.0 %fusion.121 = (f32[3,8,8,128]{3,2,1,0:T(8,128)S(1)}, f32[3,8,8,128]{3,2,1,0:T(8,128)S(1)}) fusion(f32[27,8,8,128]{3,2,1,0:T(8,128)} %param.19), kind=kLoop, calls=%fused_computation.539 | loop fusion | bytes 393216 | tf_op jit(solution)/shard_map/slice | solution.py:98
  8.3 2.6 %multiply_reduce_fusion.16 = (f32[8,8,128]{2,1,0:T(8,128)}, f32[8,8,128]{2,1,0:T(8,128)}, f32[8,8,128]{2,1,0:T(8,128)}, f32[8,8,128]{2,1,0:T(8,128)}, f32[8,8,128]{2,1,0:T(8,128)}, /*index=5*/f32[8,8,128]{2,1,0:T(8,128)}) fusion(f32[27]{0:T(128)} %constant.82, f32[3,27,8,8,128]{4,3,2,1,0:T(8,128)} %param.16, f32[27]{0:T(128)} %constant.84, f32[27]{0:T(128)} %constant.85), kind=kLoop, calls=%fused_computation.60 | loop fusion | flops 2605056 | bytes 1966404 | tf_op jit(solution)/shard_map/jvp()/reduce_sum | solution.py:59
  12.3 1.6 %broadcast_select_fusion.11 = f32[9,8,1,128]{3,2,1,0:T(1,128)} fusion(pred[]{:T(512)S(6)} %eq.64, f32[3,8,8,128]{3,2,1,0:T(8,128)S(1)} %get-tuple-element.165, f32[3,8,8,128]{3,2,1,0:T(8,128)S(1)} %get-tuple-element.89, f32[3,8,8,128]{3,2,1,0:T(8,128)S(1)} %get-tuple-element.192, f32[3,8,8,128]{3,2,1,0:T(8,128)S(1)} %get-tuple-element.166, ...), kind=kLoop, calls=%fused_computation.416 | loop fusion | flops 46080 | bytes 626689 | tf_op jit(solution)/shard_map/jit(_where)/select_n | solution.py:28
  13.9 1.6 %collective-permute-start.2 = (f32[9,8,1,128]{3,2,1,0:T(1,128)}, f32[9,8,1,128]{3,2,1,0:T(1,128)}, u32[]{:S(2)}, u32[]{:S(2)}) collective-permute-start(f32[9,8,1,128]{3,2,1,0:T(1,128)} %broadcast_select_fusion.11), channel_id=1, source_target_pairs={{0,4},{1,5},{2,6},{3,7},{4,0},{5,1},{6,2},{7,3},{8,12},{9,13},{10,... | collective-permute-start | bytes 110600 | tf_op jit(solution)/shard_map/ppermute | solution.py:21
  15.5 2.2 %slice_reduce_fusion = (f32[8,8,128]{2,1,0:T(8,128)}, f32[8,8,128]{2,1,0:T(8,128)S(1)}, f32[8,8,128]{2,1,0:T(8,128)}, f32[27,8,8,128]{3,2,1,0:T(8,128)}, f32[27,...) fusion(f32[3,27,8,8,128]{4,3,2,1,0:T(8,128)S(1)} %copy-done), kind=kLoop, calls=%fused_computation.72 | loop fusion | flops 638976 | bytes 5406720 | tf_op jit(solution)/shard_map/jvp()/reduce_sum | solution.py:56
  19.0 1.0 %fusion.34 = f32[9,8,8,128]{3,2,1,0:T(8,128)S(1)} fusion(f32[3,8,8,128]{3,2,1,0:T(8,128)} %copy-done.7, f32[3,8,8,128]{3,2,1,0:T(8,128)S(1)} %get-tuple-element.89, f32[3,8,8,128]{3,2,1,0:T(8,128)} %copy-done.8, f32[9,8,1,128]{3,2,1,0:T(1,128)S(1)} %get-tuple-element.189), kind=kLoop, calls=%fused_computation.145 | loop fusion | flops 221184 | bytes 626688 | tf_op jit(solution)/shard_map/concatenate | solution.py:85
  20.1 1.0 %fusion.35 = f32[9,8,8,128]{3,2,1,0:T(8,128)S(1)} fusion(f32[3,8,8,128]{3,2,1,0:T(8,128)S(1)} %get-tuple-element.166, f32[3,8,8,128]{3,2,1,0:T(8,128)S(1)} %get-tuple-element.90, f32[3,8,8,128]{3,2,1,0:T(8,128)} %get-tuple-element.191, f32[9,8,1,128]{3,2,1,0:T(1,128)S(1)} %get-tuple-element.190), kind=kLoop, calls=%fused_computation.148 | loop fusion | flops 221184 | bytes 626688 | tf_op jit(solution)/shard_map/concatenate | solution.py:88
  23.4 1.0 %slice_select_fusion.4 = (f32[9,8,8,1]{3,2,1,0:T(8,128)}, f32[9,8,8,1]{3,2,1,0:T(8,128)}) fusion(f32[9,8,8,128]{3,2,1,0:T(8,128)S(1)} %get-tuple-element.148, f32[9,8,8,128]{3,2,1,0:T(8,128)S(1)} %get-tuple-element.147, pred[]{:T(512)S(6)} %eq.62), kind=kLoop, calls=%fused_computation.295 | loop fusion | flops 1152 | bytes 9217 | tf_op jit(solution)/shard_map/jit(_where)/select_n | solution.py:28
  24.4 1.6 %collective-permute-start.4 = (f32[9,8,8,1]{3,2,1,0:T(8,128)}, f32[9,8,8,1]{3,2,1,0:T(8,128)}, u32[]{:S(2)}, u32[]{:S(2)}) collective-permute-start(f32[9,8,8,1]{3,2,1,0:T(8,128)} %get-tuple-element.105), channel_id=1, source_target_pairs={{0,1},{1,0},{2,3},{3,2},{4,5},{5,4},{6,7},{7,6},{8,9},{9,8},{10,11... | collective-permute-start | bytes 6920 | tf_op jit(solution)/shard_map/ppermute | solution.py:21
  26.0 1.5 %add_multiply_fusion.2 = (f32[8,8,128]{2,1,0:T(8,128)}, f32[8,8,128]{2,1,0:T(8,128)}, f32[8,8,128]{2,1,0:T(8,128)}, f32[8,8,128]{2,1,0:T(8,128)}, f32[8,8,128]{2...) fusion(f32[8,8,128]{2,1,0:T(8,128)} %get-tuple-element.17, ...), kind=kLoop, calls=%fused_computation.521 | loop fusion | flops 98304 | bytes 401408 | tf_op jit(solution)/shard_map/jvp()/mul | solution.py:62
  27.5 1.1 %slice.928 = f32[9,8,8,127]{3,2,1,0:T(8,128)S(1)} slice(f32[9,8,8,128]{3,2,1,0:T(8,128)} %copy-done.4), slice={[0:9], [0:8], [0:8], [1:128]} | slice | bytes 585216 | tf_op jit(solution)/shard_map/slice | solution.py:86
  28.6 5.4 %collective-permute-done.3 = f32[9,8,8,1]{3,2,1,0:T(8,128)} collective-permute-done((f32[9,8,8,1]{3,2,1,0:T(8,128)}, f32[9,8,8,1]{3,2,1,0:T(8,128)}, u32[]{:S(2)}, u32[]{:S(2)}) %collective-permute-start.3) | collective-permute-done | bytes 2336 | tf_op jit(solution)/shard_map/ppermute | solution.py:21
  34.0 1.1 %select_select_fusion.4 = (f32[9,8,8,1]{3,2,1,0:T(8,128)S(1)}, f32[9,8,8,1]{3,2,1,0:T(8,128)S(1)}) fusion(f32[9,8,8,1]{3,2,1,0:T(8,128)} %collective-permute-done.4, f32[9,8,8,1]{3,2,1,0:T(8,128)} %collective-permute-done.3, pred[]{:T(512)S(6)} %eq.69, pred[]{:T(512)S(6)} %eq.62, pred[]{:T(512)S(6)} %eq.31), kind=kLoop, calls=%fused_computation.154 | loop fusion | flops 2304 | bytes 9219 | tf_op jit(solution)/shard_map/jit(_where)/select_n | solution.py:34
  39.1 0.9 constant_dynamic-update-slice_fusion.28
  42.2 1.5 %fusion.27 = (f32[8,8,128]{2,1,0:T(8,128)S(1)}, f32[8,8,128]{2,1,0:T(8,128)S(1)}, f32[8,8,128]{2,1,0:T(8,128)S(1)}, f32[8,8,128]{2,1,0:T(8,128)S(1)}, f32[8,8,12...) fusion(f32[27,8,8,128]{3,2,1,0:T(8,128)S(1)} %constant_dynamic-update-slice_fusion.18, ...), kind=kLoop, calls=%fused_computation.102 | loop fusion | flops 7913472 | bytes 3080624 | tf_op jit(solution)/shard_map/transpose(jvp())/reduce_sum | solution.py:62
  44.4 1.5 %collective-permute-start.6 = (f32[9,1,8,128]{3,2,1,0:T(8,128)S(1)}, f32[9,1,8,128]{3,2,1,0:T(8,128)S(1)}, u32[]{:S(2)}, u32[]{:S(2)}) collective-permute-start(f32[9,1,8,128]{3,2,1,0:T(8,128)S(1)} %get-tuple-element.85), channel_id=1, source_target_pairs={{0,8},{1,9},{2,10},{3,11},{8,0},{9,1},{10,2},{11,3},{16,24},{17,25... | collective-permute-start | bytes 110600 | tf_op jit(solution)/shard_map/ppermute | solution.py:21
  46.0 2.4 %collective-permute-done.6 = f32[9,1,8,128]{3,2,1,0:T(8,128)S(1)} collective-permute-done((f32[9,1,8,128]{3,2,1,0:T(8,128)S(1)}, f32[9,1,8,128]{3,2,1,0:T(8,128)S(1)}, u32[]{:S(2)}, u32[]{:S(2)}) %collective-permute-start.6) | collective-permute-done | bytes 36896 | tf_op jit(solution)/shard_map/ppermute | solution.py:21
  48.5 1.6 %collective-permute-start.7 = (f32[9,8,1,128]{3,2,1,0:T(1,128)S(1)}, f32[9,8,1,128]{3,2,1,0:T(1,128)S(1)}, u32[]{:S(2)}, u32[]{:S(2)}) collective-permute-start(f32[9,8,1,128]{3,2,1,0:T(1,128)S(1)} %broadcast_select_fusion.8), channel_id=1, source_target_pairs={{0,4},{1,5},{2,6},{3,7},{4,0},{5,1},{6,2},{7,3},{8,12},{9,13},{10,... | collective-permute-start | bytes 110600 | tf_op jit(solution)/shard_map/ppermute | solution.py:21
  50.1 2.4 %collective-permute-done.7 = f32[9,8,1,128]{3,2,1,0:T(1,128)S(1)} collective-permute-done((f32[9,8,1,128]{3,2,1,0:T(1,128)S(1)}, f32[9,8,1,128]{3,2,1,0:T(1,128)S(1)}, u32[]{:S(2)}, u32[]{:S(2)}) %collective-permute-start.7) | collective-permute-done | bytes 36896 | tf_op jit(solution)/shard_map/ppermute | solution.py:21
  54.0 7.6 %collective-permute-done.8 = f32[9,8,8,1]{3,2,1,0:T(8,128)S(1)} collective-permute-done((f32[9,8,8,1]{3,2,1,0:T(8,128)S(1)}, f32[9,8,8,1]{3,2,1,0:T(8,128)S(1)}, u32[]{:S(2)}, u32[]{:S(2)}) %collective-permute-start.8) | collective-permute-done | bytes 2336 | tf_op jit(solution)/shard_map/ppermute | solution.py:21
  63.6 1.9 %multiply_reduce_fusion.11 = (f32[8,8,128]{2,1,0:T(8,128)S(1)}, f32[8,8,128]{2,1,0:T(8,128)S(1)}, f32[8,8,128]{2,1,0:T(8,128)S(1)}, f32[8,8,128]{2,1,0:T(8,128)S...) fusion(f32[27]{0:T(128)S(1)} %copy-done.27, ...), kind=kLoop, calls=%fused_computation.54 | loop fusion | flops 10534912 | bytes 4981168 | tf_op jit(solution)/shard_map/transpose(jvp())/reduce_sum | solution.py:60
  66.1 2.1 %collective-permute-start.11 = (f32[9,1,8,128]{3,2,1,0:T(8,128)S(1)}, f32[9,1,8,128]{3,2,1,0:T(8,128)S(1)}, u32[]{:S(2)}, u32[]{:S(2)}) collective-permute-start(f32[9,1,8,128]{3,2,1,0:T(8,128)S(1)} %get-tuple-element.76), channel_id=1, source_target_pairs={{0,8},{1,9},{2,10},{3,11},{8,0},{9,1},{10,2},{11,3},{16,24},{17,25... | collective-permute-start | bytes 110600 | tf_op jit(solution)/shard_map/ppermute | solution.py:21
  68.2 1.9 %collective-permute-done.11 = f32[9,1,8,128]{3,2,1,0:T(8,128)S(1)} collective-permute-done((f32[9,1,8,128]{3,2,1,0:T(8,128)S(1)}, f32[9,1,8,128]{3,2,1,0:T(8,128)S(1)}, u32[]{:S(2)}, u32[]{:S(2)}) %collective-permute-start.11) | collective-permute-done | bytes 36896 | tf_op jit(solution)/shard_map/ppermute | solution.py:21
  70.2 1.6 %collective-permute-start.12 = (f32[9,8,1,128]{3,2,1,0:T(1,128)S(1)}, f32[9,8,1,128]{3,2,1,0:T(1,128)S(1)}, u32[]{:S(2)}, u32[]{:S(2)}) collective-permute-start(f32[9,8,1,128]{3,2,1,0:T(1,128)S(1)} %broadcast_select_fusion.5), channel_id=1, source_target_pairs={{0,4},{1,5},{2,6},{3,7},{4,0},{5,1},{6,2},{7,3},{8,12},{9,13},{10,... | collective-permute-start | bytes 110600 | tf_op jit(solution)/shard_map/ppermute | solution.py:21
  71.8 2.4 %collective-permute-done.12 = f32[9,8,1,128]{3,2,1,0:T(1,128)S(1)} collective-permute-done((f32[9,8,1,128]{3,2,1,0:T(1,128)S(1)}, f32[9,8,1,128]{3,2,1,0:T(1,128)S(1)}, u32[]{:S(2)}, u32[]{:S(2)}) %collective-permute-start.12) | collective-permute-done | bytes 36896 | tf_op jit(solution)/shard_map/ppermute | solution.py:21
  74.8 1.6 %collective-permute-start.14 = (f32[9,8,8,1]{3,2,1,0:T(8,128)S(1)}, f32[9,8,8,1]{3,2,1,0:T(8,128)S(1)}, u32[]{:S(2)}, u32[]{:S(2)}) collective-permute-start(f32[9,8,8,1]{3,2,1,0:T(8,128)S(1)} %get-tuple-element.97), channel_id=1, source_target_pairs={{0,1},{1,0},{2,3},{3,2},{4,5},{5,4},{6,7},{7,6},{8,9},{9,8},{10,11... | collective-permute-start | bytes 6920 | tf_op jit(solution)/shard_map/ppermute | solution.py:21
  76.6 7.5 %collective-permute-done.13 = f32[9,8,8,1]{3,2,1,0:T(8,128)S(1)} collective-permute-done((f32[9,8,8,1]{3,2,1,0:T(8,128)S(1)}, f32[9,8,8,1]{3,2,1,0:T(8,128)S(1)}, u32[]{:S(2)}, u32[]{:S(2)}) %collective-permute-start.13) | collective-permute-done | bytes 2336 | tf_op jit(solution)/shard_map/ppermute | solution.py:21
  85.8 2.5 %fusion.4 = (f32[8,8,128]{2,1,0:T(8,128)S(1)}, f32[8,8,128]{2,1,0:T(8,128)S(1)}, f32[8,8,128]{2,1,0:T(8,128)S(1)}, f32[8,8,128]{2,1,0:T(8,128)S(1)}, f32[27,8,8,128]{3,2,1,0:T(8,128)S(1)}) fusion(f32[27,8,8,128]{3,2,1,0:T(8,128)S(1)} %constant_dynamic-update-slice_fusion.18, f32[8,8,128]{2,1,0:T(8,128)S(1)} %copy-done.19, f32[8,8,128]{2,1,0:T(8,128)S(1)} %copy-done.16, ...), kind=kLoop, calls=%fused_computation.16 | loop fusion | flops 11247616 | bytes 4915632 | tf_op jit(solution)/shard_map/transpose(jvp())/reduce_sum | solution.py:64
  88.6 1.4 %multiply_reduce_fusion = (f32[8,8,128]{2,1,0:T(8,128)S(1)}, f32[27,8,8,128]{3,2,1,0:T(8,128)}) fusion(f32[27,8,8,128]{3,2,1,0:T(8,128)S(1)} %constant_dynamic-update-slice_fusion.108, f32[27,8,8,128]{3,2,1,0:T(8,128)S(1)} %copy-done.1, f32[8,8,128]{2,1,0:T(8,128)S(1)} %get-tuple-element.168, f32[27]{0:T(128)S(1)} %copy-done.27, ...), kind=kLoop, calls=%fused_computation.39 | loop fusion | flops 3088384 | bytes 3735876 | tf_op jit(solution)/shard_map/transpose(jvp())/reduce_sum | solution.py:64
  (221 shorter events, 19.5 us)
Async XLA Ops:
  0.6 14.8 %copy-start = (f32[3,27,8,8,128]{4,3,2,1,0:T(8,128)S(1)}, f32[3,27,8,8,128]{4,3,2,1,0:T(8,128)}, u32[]{:S(2)}) copy-start(f32[3,27,8,8,128]{4,3,2,1,0:T(8,128)} %param.16) | copy-start | bytes 7962628
  1.6 9.4 %collective-permute-start = (f32[9,1,8,128]{3,2,1,0:T(8,128)S(1)}, f32[9,1,8,128]{3,2,1,0:T(8,128)S(1)}, u32[]{:S(2)}, u32[]{:S(2)}) collective-permute-start(f32[9,1,8,128]{3,2,1,0:T(8,128)S(1)} %get-tuple-element.93), channel_id=1, source_target_pairs={{0,1},{1,0},{2,3},{3,2},{8,16},{9,17},{10,18},{11,19},{16,8},{17,9... | collective-permute-start | bytes 110600 | tf_op jit(solution)/shard_map/ppermute | solution.py:21
  2.1 8.9 %collective-permute-start.1 = (f32[9,1,8,128]{3,2,1,0:T(8,128)S(1)}, f32[9,1,8,128]{3,2,1,0:T(8,128)S(1)}, u32[]{:S(2)}, u32[]{:S(2)}) collective-permute-start(f32[9,1,8,128]{3,2,1,0:T(8,128)S(1)} %get-tuple-element.94), channel_id=1, source_target_pairs={{0,8},{1,9},{2,10},{3,11},{8,0},{9,1},{10,2},{11,3},{16,24},{17,25... | collective-permute-start | bytes 110600 | tf_op jit(solution)/shard_map/ppermute | solution.py:21
  13.9 4.3 %collective-permute-start.2 = (f32[9,8,1,128]{3,2,1,0:T(1,128)}, f32[9,8,1,128]{3,2,1,0:T(1,128)}, u32[]{:S(2)}, u32[]{:S(2)}) collective-permute-start(f32[9,8,1,128]{3,2,1,0:T(1,128)} %broadcast_select_fusion.11), channel_id=1, source_target_pairs={{0,4},{1,5},{2,6},{3,7},{4,0},{5,1},{6,2},{7,3},{8,12},{9,13},{10,... | collective-permute-start | bytes 110600 | tf_op jit(solution)/shard_map/ppermute | solution.py:21
  20.1 5.9 %copy-start.5 = (f32[9,8,8,128]{3,2,1,0:T(8,128)}, f32[9,8,8,128]{3,2,1,0:T(8,128)S(1)}, u32[]{:S(2)}) copy-start(f32[9,8,8,128]{3,2,1,0:T(8,128)S(1)} %fusion.34) | copy-start | bytes 884740
  21.1 4.9 %copy-start.6 = (f32[9,8,8,128]{3,2,1,0:T(8,128)}, f32[9,8,8,128]{3,2,1,0:T(8,128)S(1)}, u32[]{:S(2)}) copy-start(f32[9,8,8,128]{3,2,1,0:T(8,128)S(1)} %fusion.35) | copy-start | bytes 884740
  24.4 9.6 %collective-permute-start.3 = (f32[9,8,8,1]{3,2,1,0:T(8,128)}, f32[9,8,8,1]{3,2,1,0:T(8,128)}, u32[]{:S(2)}, u32[]{:S(2)}) collective-permute-start(f32[9,8,8,1]{3,2,1,0:T(8,128)} %get-tuple-element.106), channel_id=1, source_target_pairs={{0,3},{1,2},{2,1},{3,0},{4,7},{5,6},{6,5},{7,4},{8,11},{9,10},{10,... | collective-permute-start | bytes 6920 | tf_op jit(solution)/shard_map/ppermute | solution.py:21
  24.4 9.6 %collective-permute-start.4 = (f32[9,8,8,1]{3,2,1,0:T(8,128)}, f32[9,8,8,1]{3,2,1,0:T(8,128)}, u32[]{:S(2)}, u32[]{:S(2)}) collective-permute-start(f32[9,8,8,1]{3,2,1,0:T(8,128)} %get-tuple-element.105), channel_id=1, source_target_pairs={{0,1},{1,0},{2,3},{3,2},{4,5},{5,4},{6,7},{7,6},{8,9},{9,8},{10,11... | collective-permute-start | bytes 6920 | tf_op jit(solution)/shard_map/ppermute | solution.py:21
  27.5 8.6 %copy-start.12 = (f32[9,1,8,128]{3,2,1,0:T(8,128)S(1)}, f32[9,1,8,128]{3,2,1,0:T(8,128)}, u32[]{:S(2)}) copy-start(f32[9,1,8,128]{3,2,1,0:T(8,128)} %copy-done.11) | copy-start | bytes 110596
  37.2 3.9 %copy-start.10 = (f32[9,1,8,128]{3,2,1,0:T(8,128)S(1)}, f32[9,1,8,128]{3,2,1,0:T(8,128)}, u32[]{:S(2)}) copy-start(f32[9,1,8,128]{3,2,1,0:T(8,128)} %copy-done.9) | copy-start | bytes 110596
  39.0 3.2 %copy-start.2 = (f32[27,8,8,128]{3,2,1,0:T(8,128)S(1)}, f32[27,8,8,128]{3,2,1,0:T(8,128)}, u32[]{:S(2)}) copy-start(f32[27,8,8,128]{3,2,1,0:T(8,128)} %get-tuple-element.65) | copy-start | bytes 2654212
  39.0 3.2 %copy-start.13 = (f32[8,8,128]{2,1,0:T(8,128)S(1)}, f32[8,8,128]{2,1,0:T(8,128)}, u32[]{:S(2)}) copy-start(f32[8,8,128]{2,1,0:T(8,128)} %get-tuple-element.194) | copy-start | bytes 98308
  39.0 3.2 %copy-start.14 = (f32[8,8,128]{2,1,0:T(8,128)S(1)}, f32[8,8,128]{2,1,0:T(8,128)}, u32[]{:S(2)}) copy-start(f32[8,8,128]{2,1,0:T(8,128)} %get-tuple-element.57) | copy-start | bytes 98308
  39.0 3.2 %copy-start.15 = (f32[8,8,128]{2,1,0:T(8,128)S(1)}, f32[8,8,128]{2,1,0:T(8,128)}, u32[]{:S(2)}) copy-start(f32[8,8,128]{2,1,0:T(8,128)} %get-tuple-element.58) | copy-start | bytes 98308
  39.0 3.2 %copy-start.16 = (f32[8,8,128]{2,1,0:T(8,128)S(1)}, f32[8,8,128]{2,1,0:T(8,128)}, u32[]{:S(2)}) copy-start(f32[8,8,128]{2,1,0:T(8,128)} %get-tuple-element.59) | copy-start | bytes 98308
  39.0 3.2 %copy-start.19 = (f32[8,8,128]{2,1,0:T(8,128)S(1)}, f32[8,8,128]{2,1,0:T(8,128)}, u32[]{:S(2)}) copy-start(f32[8,8,128]{2,1,0:T(8,128)} %get-tuple-element.56) | copy-start | bytes 98308
  39.0 3.2 %copy-start.26 = (f32[27]{0:T(128)S(1)}, f32[27]{0:T(128)}, u32[]{:S(2)}) copy-start(f32[27]{0:T(128)} %constant.82) | copy-start | bytes 328
  44.2 1.7 %collective-permute-start.5 = (f32[9,1,8,128]{3,2,1,0:T(8,128)S(1)}, f32[9,1,8,128]{3,2,1,0:T(8,128)S(1)}, u32[]{:S(2)}, u32[]{:S(2)}) collective-permute-start(f32[9,1,8,128]{3,2,1,0:T(8,128)S(1)} %get-tuple-element.84), channel_id=1, source_target_pairs={{0,1},{1,0},{2,3},{3,2},{8,16},{9,17},{10,18},{11,19},{16,8},{17,9... | collective-permute-start | bytes 110600 | tf_op jit(solution)/shard_map/ppermute | solution.py:21
  44.4 4.0 %collective-permute-start.6 = (f32[9,1,8,128]{3,2,1,0:T(8,128)S(1)}, f32[9,1,8,128]{3,2,1,0:T(8,128)S(1)}, u32[]{:S(2)}, u32[]{:S(2)}) collective-permute-start(f32[9,1,8,128]{3,2,1,0:T(8,128)S(1)} %get-tuple-element.85), channel_id=1, source_target_pairs={{0,8},{1,9},{2,10},{3,11},{8,0},{9,1},{10,2},{11,3},{16,24},{17,25... | collective-permute-start | bytes 110600 | tf_op jit(solution)/shard_map/ppermute | solution.py:21
  48.4 5.4 %copy-start.18 = (f32[8,8,128]{2,1,0:T(8,128)S(1)}, f32[8,8,128]{2,1,0:T(8,128)}, u32[]{:S(2)}) copy-start(f32[8,8,128]{2,1,0:T(8,128)} %get-tuple-element.16) | copy-start | bytes 98308
  48.4 5.4 %copy-start.23 = (f32[8,8,128]{2,1,0:T(8,128)S(1)}, f32[8,8,128]{2,1,0:T(8,128)}, u32[]{:S(2)}) copy-start(f32[8,8,128]{2,1,0:T(8,128)} %get-tuple-element.8) | copy-start | bytes 98308
  48.4 5.4 %copy-start.24 = (f32[8,8,128]{2,1,0:T(8,128)S(1)}, f32[8,8,128]{2,1,0:T(8,128)}, u32[]{:S(2)}) copy-start(f32[8,8,128]{2,1,0:T(8,128)} %get-tuple-element.18) | copy-start | bytes 98308
  48.4 5.4 %copy-start.25 = (f32[8,8,128]{2,1,0:T(8,128)S(1)}, f32[8,8,128]{2,1,0:T(8,128)}, u32[]{:S(2)}) copy-start(f32[8,8,128]{2,1,0:T(8,128)} %get-tuple-element.20) | copy-start | bytes 98308
  48.5 4.0 %collective-permute-start.7 = (f32[9,8,1,128]{3,2,1,0:T(1,128)S(1)}, f32[9,8,1,128]{3,2,1,0:T(1,128)S(1)}, u32[]{:S(2)}, u32[]{:S(2)}) collective-permute-start(f32[9,8,1,128]{3,2,1,0:T(1,128)S(1)} %broadcast_select_fusion.8), channel_id=1, source_target_pairs={{0,4},{1,5},{2,6},{3,7},{4,0},{5,1},{6,2},{7,3},{8,12},{9,13},{10,... | collective-permute-start | bytes 110600 | tf_op jit(solution)/shard_map/ppermute | solution.py:21
  53.0 8.5 %collective-permute-start.8 = (f32[9,8,8,1]{3,2,1,0:T(8,128)S(1)}, f32[9,8,8,1]{3,2,1,0:T(8,128)S(1)}, u32[]{:S(2)}, u32[]{:S(2)}) collective-permute-start(f32[9,8,8,1]{3,2,1,0:T(8,128)S(1)} %get-tuple-element.102), channel_id=1, source_target_pairs={{0,3},{1,2},{2,1},{3,0},{4,7},{5,6},{6,5},{7,4},{8,11},{9,10},{10,... | collective-permute-start | bytes 6920 | tf_op jit(solution)/shard_map/ppermute | solution.py:21
  53.1 8.4 %collective-permute-start.9 = (f32[9,8,8,1]{3,2,1,0:T(8,128)S(1)}, f32[9,8,8,1]{3,2,1,0:T(8,128)S(1)}, u32[]{:S(2)}, u32[]{:S(2)}) collective-permute-start(f32[9,8,8,1]{3,2,1,0:T(8,128)S(1)} %get-tuple-element.101), channel_id=1, source_target_pairs={{0,1},{1,0},{2,3},{3,2},{4,5},{5,4},{6,7},{7,6},{8,9},{9,8},{10,11... | collective-permute-start | bytes 6920 | tf_op jit(solution)/shard_map/ppermute | solution.py:21
  66.0 2.2 %collective-permute-start.10 = (f32[9,1,8,128]{3,2,1,0:T(8,128)S(1)}, f32[9,1,8,128]{3,2,1,0:T(8,128)S(1)}, u32[]{:S(2)}, u32[]{:S(2)}) collective-permute-start(f32[9,1,8,128]{3,2,1,0:T(8,128)S(1)} %get-tuple-element.75), channel_id=1, source_target_pairs={{0,1},{1,0},{2,3},{3,2},{8,16},{9,17},{10,18},{11,19},{16,8},{17,9... | collective-permute-start | bytes 110600 | tf_op jit(solution)/shard_map/ppermute | solution.py:21
  66.1 4.0 %collective-permute-start.11 = (f32[9,1,8,128]{3,2,1,0:T(8,128)S(1)}, f32[9,1,8,128]{3,2,1,0:T(8,128)S(1)}, u32[]{:S(2)}, u32[]{:S(2)}) collective-permute-start(f32[9,1,8,128]{3,2,1,0:T(8,128)S(1)} %get-tuple-element.76), channel_id=1, source_target_pairs={{0,8},{1,9},{2,10},{3,11},{8,0},{9,1},{10,2},{11,3},{16,24},{17,25... | collective-permute-start | bytes 110600 | tf_op jit(solution)/shard_map/ppermute | solution.py:21
  70.2 6.3 %copy-start.17 = (f32[8,8,128]{2,1,0:T(8,128)S(1)}, f32[8,8,128]{2,1,0:T(8,128)}, u32[]{:S(2)}) copy-start(f32[8,8,128]{2,1,0:T(8,128)} %get-tuple-element.14) | copy-start | bytes 98308
  70.2 4.0 %collective-permute-start.12 = (f32[9,8,1,128]{3,2,1,0:T(1,128)S(1)}, f32[9,8,1,128]{3,2,1,0:T(1,128)S(1)}, u32[]{:S(2)}, u32[]{:S(2)}) collective-permute-start(f32[9,8,1,128]{3,2,1,0:T(1,128)S(1)} %broadcast_select_fusion.5), channel_id=1, source_target_pairs={{0,4},{1,5},{2,6},{3,7},{4,0},{5,1},{6,2},{7,3},{8,12},{9,13},{10,... | collective-permute-start | bytes 110600 | tf_op jit(solution)/shard_map/ppermute | solution.py:21
  74.8 9.3 %collective-permute-start.13 = (f32[9,8,8,1]{3,2,1,0:T(8,128)S(1)}, f32[9,8,8,1]{3,2,1,0:T(8,128)S(1)}, u32[]{:S(2)}, u32[]{:S(2)}) collective-permute-start(f32[9,8,8,1]{3,2,1,0:T(8,128)S(1)} %get-tuple-element.98), channel_id=1, source_target_pairs={{0,3},{1,2},{2,1},{3,0},{4,7},{5,6},{6,5},{7,4},{8,11},{9,10},{10,... | collective-permute-start | bytes 6920 | tf_op jit(solution)/shard_map/ppermute | solution.py:21
  74.8 9.3 %collective-permute-start.14 = (f32[9,8,8,1]{3,2,1,0:T(8,128)S(1)}, f32[9,8,8,1]{3,2,1,0:T(8,128)S(1)}, u32[]{:S(2)}, u32[]{:S(2)}) collective-permute-start(f32[9,8,8,1]{3,2,1,0:T(8,128)S(1)} %get-tuple-element.97), channel_id=1, source_target_pairs={{0,1},{1,0},{2,3},{3,2},{4,5},{5,4},{6,7},{7,6},{8,9},{9,8},{10,11... | collective-permute-start | bytes 6920 | tf_op jit(solution)/shard_map/ppermute | solution.py:21
  (13 other events, 32.5 us)

commit v2 on v1

v2 whole, which is shorter than its diff:
```python
import functools

import jax
import jax.numpy as jnp
import numpy as np
from jax import lax
from jax.experimental import pallas as pl
from jax.experimental.pallas import tpu as pltpu
from jax.sharding import PartitionSpec as P

STEPS = 3
DEPTH = STEPS
SLOTS = 8
Q = 27

VEL = np.array([[a, b, c] for a in (-1, 0, 1) for b in (-1, 0, 1) for c in (-1, 0, 1)])


def pop(cx, cy, cz):
    return 9 * (cx + 1) + 3 * (cy + 1) + cz + 1


U2, U1, SOLID, FLUIDITY = 27, 30, 33, 34
TRAVEL = 34


def reach(quantity, dim, toward):
    if quantity < Q:
        return DEPTH - 1 - int(VEL[quantity, dim]) * toward
    return 1 if U1 <= quantity < U1 + 3 else 2


def mirrored(quantity, dim):
    if quantity >= Q:
        return quantity
    c = [int(v) for v in VEL[quantity]]
    c[dim] = -c[dim]
    return pop(*c)


UPWARD = [(q, p) for q in range(TRAVEL) for p in range(1, reach(q, 0, 1) + 1)]


def swapped(value, axis, odd, spare):
    length = lax.axis_size(axis)
    wide = lax.axis_size(spare) if spare else 1
    pairs = []
    for i in range(length):
        for k in range(wide):
            j, m = ((i + 1 if i % 2 == 1 else i - 1) if odd else i ^ 1), k
            if not 0 <= j < length:
                j, m = (i, k ^ 1) if spare else (j % length, k)
            if j < length and m < wide:
                pairs.append((i * wide + k, j * wide + m))
    return lax.ppermute(value, (axis, spare) if spare else axis, pairs)


def both_matchings(first, second, axis, spare):
    a = swapped(first, axis, False, spare)
    return a, (swapped(second, axis, True, spare) if lax.axis_size(axis) > 2 else a)


class Place:
    def __init__(self, axis):
        index = lax.axis_index(axis)
        self.even = lax.rem(index, 2) == 0
        self.lower = index > 0
        self.upper = index < lax.axis_size(axis) - 1

    def send(self, up, down):
        return jnp.where(self.even, up, down), jnp.where(self.even, down, up)

    def take(self, first, second):
        below = jnp.where(self.even, second, first)
        above = jnp.where(self.even, first, second)
        zero = jnp.zeros_like(first)
        return jnp.where(self.lower, below, zero), jnp.where(self.upper, above, zero)


class Shape:
    def __init__(self, nx, ny, nz):
        self.nx, self.ny, self.nz = nx, ny, nz
        self.rows = 2 * 8 * -(-(nx + 2 * DEPTH + 1) // 16)
        self.halo = nx + 2 * DEPTH
        if self.halo * SLOTS > nz or nx * SLOTS * 2 > nz or nx < DEPTH or ny != 8 or nz < 6:
            raise ValueError("local block")

    def at(self, quantity, row):
        start = (quantity * self.rows + row) * self.ny
        if not isinstance(start, int):
            start = pl.multiple_of(start, self.ny)
        return pl.ds(start, self.ny)

    def raw(self, quantity, x):
        start = (quantity * self.nx + x) * self.ny
        if not isinstance(start, int):
            start = pl.multiple_of(start, self.ny)
        return pl.ds(start, self.ny)

    def tile(self, index):
        return pl.ds(index * self.ny, self.ny)


def lanes(g):
    return lax.broadcasted_iota(jnp.int32, (g.ny, g.nz), 1)


def roll(value, by, axis):
    size = value.shape[axis]
    if isinstance(by, int):
        by = by % size
        if by == 0:
            return value
    return pltpu.roll(value, by, axis)


def moments(load):
    total, my, mz, sums = [], [], [], {}
    for a in (-1, 0, 1):
        t, z = [], []
        for b in (-1, 0, 1):
            low, mid, high = (load(pop(a, b, c)) for c in (-1, 0, 1))
            t.append(low + mid + high)
            z.append(high - low)
        total.append(t[0] + t[1] + t[2])
        my.append(t[2] - t[0])
        mz.append(z[0] + z[1] + z[2])
    return (
        total[0] + total[1] + total[2],
        total[2] - total[0],
        my[0] + my[1] + my[2],
        mz[0] + mz[1] + mz[2],
    )


def velocity(load):
    rho, mx, my, mz = moments(load)
    inverse = 1.0 / rho
    return rho, mx * inverse, my * inverse, mz * inverse


def open_kernel(g, seed, saved, porosity, fluid, za, zb, xa, xb, mom):
    nx = g.nx

    def row(x, carry):
        here = pl.ds(pl.multiple_of(x * g.ny, g.ny), g.ny)
        mom[g.raw(8, x), :] = jnp.where(fluid[here, :] == 1, porosity[here, :], 1.0)
        for step, base in ((2, 0), (1, 4)):
            found = velocity(lambda i: saved[g.raw(step * Q + i, x), :])
            for k in range(4):
                mom[g.raw(base + k, x), :] = found[k]
        return carry

    lax.fori_loop(0, nx, row, 0)

    def source(q, x):
        if q < Q:
            return seed[g.raw(q, x), :]
        return mom[g.raw({U2: 1, U1: 5, SOLID: 8}[q - q % 3 if q < SOLID else q] + (q % 3 if q < SOLID else 0), x), :]

    lane = lanes(g)
    group, offset = lane // SLOTS, lane % SLOTS
    joint = []
    for q in range(TRAVEL):
        half = (q % 2) * nx
        acc = joint.pop() if q % 2 else jnp.zeros((g.ny, g.nz), jnp.float32)
        for x in range(nx):
            moved = roll(source(q, x), (half + x) * SLOTS + DEPTH, 1)
            acc = jnp.where(group == half + x, moved, acc)
        joint.append(acc)
    z = Place("gz")
    if len(joint) % 2:
        joint.append(joint[-1])
    for k in range(len(joint) // 2):
        first, second = joint[2 * k], joint[2 * k + 1]
        up = jnp.where(offset < 4, first, roll(second, 4, 1))
        down = jnp.where(offset < 4, roll(first, -3, 1), roll(second, 1, 1))
        za[g.tile(k), :], zb[g.tile(k), :] = z.send(up, down)

    x = Place("gx")
    for k, (q, p) in enumerate(UPWARD):
        xa[g.tile(k), :], xb[g.tile(k), :] = x.send(source(q, nx - p), source(mirrored(q, 0), p - 1))


def swap_edges(g, field, i, row):
    lane = lanes(g)
    cz = int(VEL[i, 2])
    if cz == 0:
        return
    own, edge, slot = field[g.at(i, row), :], field[g.at(i, g.halo), :], row * SLOTS
    if cz > 0:
        here, out, back = 0, slot + DEPTH + 2, slot + DEPTH
    else:
        here, out, back = g.nz - 1, slot + DEPTH - 1, slot + DEPTH + 1
    field[g.at(i, row), :] = jnp.where(lane == here, roll(edge, here - out + g.nz, 1), own)
    field[g.at(i, g.halo), :] = jnp.where(lane == back, roll(own, back - here + g.nz, 1), edge)


def second_kernel(g, seed, mom, za, zb, sa, sb, field, extra):
    nx = g.nx
    lane = lanes(g)
    group, offset = lane // SLOTS, lane % SLOTS
    inner = (group >= DEPTH) & (group < DEPTH + nx)
    z = Place("gz")

    def target(q):
        return (field, q) if q < Q else (extra, q - Q)

    below, above = [], []
    for k in range(-(-TRAVEL // 4)):
        low, high = z.take(za[g.tile(k), :], zb[g.tile(k), :])
        below.append(low)
        above.append(high)
    halo = []
    for q in range(TRAVEL):
        at = (q % 2) * nx * SLOTS + (q // 2 % 2) * 4
        low = roll(below[q // 4], DEPTH * SLOTS - at, 1)
        high = roll(above[q // 4], DEPTH * SLOTS + DEPTH + 2 - at, 1)
        tile = jnp.where(offset < 4, low, high)
        halo.append(jnp.where(inner, tile, 0.0))
        ref, index = target(q)
        ref[g.at(index, g.halo), :] = halo[-1]
    x = Place("gx")
    width = DEPTH * SLOTS
    per = g.nz // width
    for k in range(-(-TRAVEL // per)):
        up = down = jnp.zeros((g.ny, g.nz), jnp.float32)
        for j in range(min(per, TRAVEL - k * per)):
            tile = halo[k * per + j]
            part = (lane >= j * width) & (lane < (j + 1) * width)
            up = jnp.where(part, roll(tile, j * width - nx * SLOTS, 1), up)
            down = jnp.where(part, roll(tile, j * width - DEPTH * SLOTS, 1), down)
        sa[g.tile(k), :], sb[g.tile(k), :] = x.send(up, down)

    def row(r, carry):
        for i in range(Q):
            field[g.at(i, r + DEPTH), :] = seed[g.raw(i, r), :]
            swap_edges(g, field, i, r + DEPTH)
        for k in range(3):
            extra[g.at(k, r + DEPTH), :] = mom[g.raw(1 + k, r), :]
            extra[g.at(3 + k, r + DEPTH), :] = mom[g.raw(5 + k, r), :]
        solid = mom[g.raw(8, r), :]
        extra[g.at(6, r + DEPTH), :] = solid
        extra[g.at(7, r + DEPTH), :] = 1.0 - solid
        return carry

    lax.fori_loop(0, nx, row, 0)


def y_message(g, field, ya, yb):
    y = Place("gy")
    for k in range(9):
        a, c = k // 3 - 1, k % 3 - 1
        for half in range(g.rows // 8):
            def line(i, edge):
                return field[pl.ds((i * g.rows + half * 8) * g.ny + edge, 8, stride=g.ny), :]
            here = pl.ds(k * g.rows + half * 8, 8)
            ya[here, :], yb[here, :] = y.send(line(pop(a, -1, c), g.ny - 1), line(pop(a, 1, c), 0))


def third_kernel(g, field, extra, xa, xb, sa, sb, field_out, extra_out, ya, yb):
    del field, extra
    nx = g.nx
    x, z = Place("gx"), Place("gz")
    lane = lanes(g)
    group, offset = lane // SLOTS, lane % SLOTS

    def target(q):
        return (field_out, q) if q < Q else (extra_out, q - Q)

    for k, (q, p) in enumerate(UPWARD):
        low, high = x.take(xa[g.tile(k), :], xb[g.tile(k), :])
        ref, index = target(q)
        ref[g.at(index, DEPTH - p), :] = low
        ref, index = target(mirrored(q, 0))
        ref[g.at(index, DEPTH + nx - 1 + p), :] = high
        if q == SOLID:
            extra_out[g.at(7, DEPTH - p), :] = jnp.where(x.lower, 1.0 - low, 0.0)
            extra_out[g.at(7, DEPTH + nx - 1 + p), :] = jnp.where(x.upper, 1.0 - high, 0.0)
    width = DEPTH * SLOTS
    per = g.nz // width
    for k in range(-(-TRAVEL // per)):
        low, high = x.take(sa[g.tile(k), :], sb[g.tile(k), :])
        for j in range(min(per, TRAVEL - k * per)):
            ref, index = target(k * per + j)
            tile = ref[g.at(index, g.halo), :]
            tile = jnp.where(group < DEPTH, roll(low, -j * width, 1), tile)
            tile = jnp.where(group >= DEPTH + nx, roll(high, (DEPTH + nx) * SLOTS - j * width, 1), tile)
            ref[g.at(index, g.halo), :] = tile
    there = jnp.where(group < DEPTH, jnp.where(x.lower, 1, 0), jnp.where(group >= DEPTH + nx, jnp.where(x.upper, 1, 0), 1))
    there = there * jnp.where(offset < 4, jnp.where(z.lower, 1, 0), jnp.where(z.upper, 1, 0))
    extra_out[g.at(7, g.halo), :] = jnp.where(there == 1, 1.0 - extra_out[g.at(6, g.halo), :], 0.0)

    for side in (0, DEPTH + nx):
        for i in range(Q):
            for r in range(side, side + DEPTH):
                swap_edges(g, field_out, i, r)
    y_message(g, field_out, ya, yb)


def pulled_moments(p):
    t = {}
    for a in (-1, 0, 1):
        s0, s1, s2 = [], [], []
        for b in (-1, 0, 1):
            low, mid, high = (p[pop(a, b, c)] for c in (-1, 0, 1))
            both = low + high
            s0.append(4.0 * mid + both)
            s1.append(high - low)
            s2.append(both)
        both = s0[0] + s0[2]
        t[a] = (
            4.0 * s0[1] + both,
            s0[2] - s0[0],
            both,
            4.0 * s1[1] + (s1[0] + s1[2]),
            s1[2] - s1[0],
            4.0 * s2[1] + (s2[0] + s2[2]),
        )
    both = [t[-1][k] + t[1][k] for k in range(6)]
    full = [4.0 * t[0][k] + both[k] for k in range(6)]
    m0, my, myy, mz, myz, mzz = full
    mx, mxx = t[1][0] - t[-1][0], both[0]
    mxy, mxz = t[1][1] - t[-1][1], t[1][3] - t[-1][3]
    return m0, mx, my, mz, mxx, myy, mzz, mxy, mxz, myz


def transposed(p, u, solid, fluidity):
    m0, mx, my, mz, mxx, myy, mzz, mxy, mxz, myz = pulled_moments(p)
    ux, uy, uz = u
    usq = ux * ux + uy * uy + uz * uz
    vx = mxx * ux + mxy * uy + mxz * uz
    vy = mxy * ux + myy * uy + myz * uz
    vz = mxz * ux + myz * uy + mzz * uz
    quad = ux * vx + uy * vy + uz * vz
    scale = fluidity * (1.6 / 216.0)
    kept = -0.6 * fluidity
    base = scale * (m0 + 1.5 * usq * m0 - 4.5 * quad)
    bx = scale * (3.0 * (mx - ux * m0) + 9.0 * vx)
    by = scale * (3.0 * (my - uy * m0) + 9.0 * vy)
    bz = scale * (3.0 * (mz - uz * m0) + 9.0 * vz)
    out = [None] * Q
    for a in (-1, 0, 1):
        ga = base + bx if a > 0 else (base - bx if a < 0 else base)
        for b in (-1, 0, 1):
            gb = ga + by if b > 0 else (ga - by if b < 0 else ga)
            for c in (-1, 0, 1):
                gc = gb + bz if c > 0 else (gb - bz if c < 0 else gb)
                i = pop(a, b, c)
                out[i] = kept * p[i] + solid * p[Q - 1 - i] + gc
    flow = m0 * (1.0 - 1.5 * usq) + 3.0 * (ux * mx + uy * my + uz * mz) + 4.5 * quad
    return out, flow


def step_kernel(g, step, field, extra, mom, saved, fluid, ya, yb, grad, kept, result, grad_out, *messages):
    del field
    nx = g.nx
    y = Place("gy")
    for k in range(9):
        a, c = k // 3 - 1, k % 3 - 1
        for half in range(g.rows // 8):
            here = pl.ds(k * g.rows + half * 8, 8)
            low, high = y.take(ya[here, :], yb[here, :])
            for i, edge, value in ((pop(a, -1, c), g.ny - 1, low), (pop(a, 1, c), 0, high)):
                kept[pl.ds((i * g.rows + half * 8) * g.ny + edge, 8, stride=g.ny), :] = value

    base = {2: 0, 1: 3, 0: None}[step]

    def parts(row):
        solid, fluidity = extra[g.at(6, row), :], extra[g.at(7, row), :]
        return tuple(extra[g.at(base + k, row), :] for k in range(3)), solid, fluidity

    if step:
        tile = [kept[g.at(i, g.halo), :] for i in range(Q)]
        p = [
            roll(roll(tile[i], -(SLOTS * int(VEL[i, 0]) + int(VEL[i, 2])), 1), -int(VEL[i, 1]), 0)
            for i in range(Q)
        ]
        out, _ = transposed(p, *parts(g.halo))
        for i in range(Q):
            result[g.at(i, g.halo), :] = out[i]

    def pull(row):
        return [
            roll(
                roll(kept[g.at(i, row + int(VEL[i, 0])), :], -int(VEL[i, 2]), 1),
                -int(VEL[i, 1]),
                0,
            )
            for i in range(Q)
        ]

    def store(row, out):
        for i in range(Q):
            result[g.at(i, row), :] = out[i]
            swap_edges(g, result, i, row)

    def outer(row):
        out, _ = transposed(pull(row), *parts(row))
        store(row, out)

    def inner(x, carry):
        row = x + DEPTH
        here = pl.ds(pl.multiple_of(x * g.ny, g.ny), g.ny)
        p = pull(row)
        if step:
            u, solid, fluidity = parts(row)
            rho = mom[g.raw(4 * (2 - step), x), :]
        else:
            rho, *u = velocity(lambda i: saved[g.raw(i, x), :])
            solid, fluidity = extra[g.at(6, row), :], extra[g.at(7, row), :]
        out, flow = transposed(p, u, solid, fluidity)
        same = cross = None
        for i in range(Q):
            f = saved[g.raw(step * Q + i, x), :]
            one, two = p[i] * f, p[Q - 1 - i] * f
            same, cross = (one, two) if same is None else (same + one, cross + two)
        term = 0.6 * same + cross - (1.6 / 216.0) * (rho * flow)
        grad_out[here, :] = jnp.where(fluid[here, :] == 1, grad[here, :] + term, 0.0)
        if step:
            store(row, out)
        else:
            for i in range(Q):
                result[g.raw(i, x), :] = out[i]
        return carry

    lax.fori_loop(0, nx, inner, 0)
    if step:
        for r in range(DEPTH - step + 1 - 1, DEPTH):
            if r >= STEPS - step:
                outer(r)
        for r in range(DEPTH + nx, DEPTH + nx + step):
            if r < DEPTH + nx + step - 0:
                outer(r)
        y_message(g, result, *messages)


def call(kernel, name, outs, args, flops, aliases=None):
    moved = 4 * sum(int(np.prod(a.shape)) for a in [*args, *outs])
    return pl.pallas_call(
        kernel,
        name=name,
        out_shape=[jax.ShapeDtypeStruct(o, jnp.float32) if isinstance(o, tuple) else o for o in outs],
        in_specs=[pl.BlockSpec(memory_space=pltpu.VMEM)] * len(args),
        out_specs=[pl.BlockSpec(memory_space=pltpu.VMEM)] * len(outs),
        input_output_aliases=aliases or {},
        compiler_params=pltpu.CompilerParams(vmem_limit_bytes=VMEM_LIMIT),
        cost_estimate=pl.CostEstimate(flops=flops, bytes_accessed=moved, transcendentals=0),
    )(*args)


VMEM_LIMIT = 24 * 1024 * 1024


def local(saved, porosity, fluid, seed_adjoint):
    nx, ny, nz = porosity.shape
    g = Shape(nx, ny, nz)
    f32 = lambda *shape: jax.ShapeDtypeStruct(shape, jnp.float32)
    seed = seed_adjoint.reshape(Q * nx * ny, nz)
    pops = saved.reshape(STEPS * Q * nx * ny, nz)
    porosity = porosity.reshape(nx * ny, nz)
    fluid = fluid.reshape(nx * ny, nz)
    voxels = nx * ny * nz

    zs = f32(-(-TRAVEL // 4) * ny, nz)
    xs = f32(len(UPWARD) * ny, nz)
    za, zb, xa, xb, mom = call(
        functools.partial(open_kernel, g), "open", [zs, zs, xs, xs, f32(9 * nx * ny, nz)],
        [seed, pops, porosity, fluid], 200 * voxels,
    )
    za, zb = both_matchings(za, zb, "gz", None)
    xa, xb = both_matchings(xa, xb, "gx", "gz")
    per = nz // (DEPTH * SLOTS)
    ss = f32(-(-TRAVEL // per) * ny, nz)
    whole, more = f32(Q * g.rows * ny, nz), f32(8 * g.rows * ny, nz)
    sa, sb, field, extra = call(
        functools.partial(second_kernel, g), "second", [ss, ss, whole, more], [seed, mom, za, zb], 100 * voxels
    )
    sa, sb = both_matchings(sa, sb, "gx", "gz")
    ys = f32(9 * g.rows, nz)
    field, extra, ya, yb = call(
        functools.partial(third_kernel, g), "third", [whole, more, ys, ys],
        [field, extra, xa, xb, sa, sb], 100 * voxels, {0: 0, 1: 1},
    )
    grad = jnp.zeros((nx * ny, nz), jnp.float32)
    flat = f32(nx * ny, nz)
    for step in (2, 1):
        ya, yb = both_matchings(ya, yb, "gy", "gz")
        _, field, grad, ya, yb = call(
            functools.partial(step_kernel, g, step), f"step{step}", [whole, whole, flat, ys, ys],
            [field, extra, mom, pops, fluid, ya, yb, grad], 400 * voxels, {0: 0},
        )
    ya, yb = both_matchings(ya, yb, "gy", "gz")
    _, adjoint, grad = call(
        functools.partial(step_kernel, g, 0), "step0", [whole, f32(Q * nx * ny, nz), flat],
        [field, extra, mom, pops, fluid, ya, yb, grad], 400 * voxels, {0: 0},
    )
    return adjoint.reshape(Q, nx, ny, nz), grad.reshape(nx, ny, nz)


def solution(mesh):
    return jax.shard_map(
        local,
        mesh=mesh,
        in_specs=(
            P(None, None, "gx", "gy", "gz"),
            P("gx", "gy", "gz"),
            P("gx", "gy", "gz"),
            P(None, "gx", "gy", "gz"),
        ),
        out_specs=(P(None, "gx", "gy", "gz"), P("gx", "gy", "gz")),
        check_vma=False,
    )
```

time: 91.7 us -> 69.1 us (0.75)
  Pallas kernels: 0 us -> 38.9 us
  other arithmetic: 30.3 us -> 0 us
  waiting for transfers between devices: 30.2 us -> 12.5 us
  local copies, waits for them, and re-layouts: 11.3 us -> 4.44 us
  starting transfers between devices: 17.3 us -> 12.2 us
  between operations: 1.61 us -> 0.66 us
    pallas_call x0 -> x6, Pallas kernels: none -> 38.9 us  [call(): pl.pallas_call(kernel, name=name, out_shape=[jax.ShapeDtypeStruct(o, jnp....]
    ppermute x15 -> x9, waiting for transfers between devices: 30.2 us -> 12.5 us  [swapped(): return lax.ppermute(value, (axis, spare) if spare else axis, pairs)]
    reduce_sum x7 -> x0, other arithmetic: 12.3 us -> none  [the longest x2 3.82 us: collide(): return (1.0 - solid) * relaxed + solid * pops[::-1]]
    select_n x18 -> x0, other arithmetic: 6.11 us -> none  [the longest x6 2.95 us: exchanged(): first = swapped(jnp.where(even, to_upper, to_lower), axis, False, spare)]
    unnamed x63 -> x0, other arithmetic: 5.42 us -> none
    ppermute x15 -> x9, starting transfers between devices: 17.3 us -> 12.2 us  [swapped(): return lax.ppermute(value, (axis, spare) if spare else axis, pairs)]
    slice x9 -> x0, local copies, waits for them, and re-layouts: 3.53 us -> none  [the longest x3 1.36 us: move_along(): jax.lax.slice_in_dim(going_up, 1, length, axis=dim)]
    unnamed x99 -> x12, local copies, waits for them, and re-layouts: 7.72 us -> 4.43 us
  transfers between devices with their start and end apart: 15 -> 9, of which waited for: 8 -> 5; matrix products, arithmetic and copies ran while one was open for 11% -> 0% of each run, Pallas kernels for 0% -> 15%
where the time goes in v2:
time: 69.1 us; the launch traced here: 68.8 us
  Pallas kernels  38.9 us (56%)
  waiting for transfers between devices  12.5 us (18%)
  starting transfers between devices  12.2 us (18%)
  local copies, waits for them, and re-layouts  4.44 us (6%)
    pallas_call x6, Pallas kernels, call(): pl.pallas_call(kernel, name=name, out_shape=[jax.ShapeDtypeStruct(o, jnp....  38.9 us
    ppermute x9, waiting for transfers between devices, swapped(): return lax.ppermute(value, (axis, spare) if spare else axis, pairs)  12.5 us
    ppermute x9, starting transfers between devices, swapped(): return lax.ppermute(value, (axis, spare) if spare else axis, pairs)  12.2 us
    unnamed x12, local copies, waits for them, and re-layouts  4.43 us
  transfers between devices with their start and end apart: 9, of which 5 were waited for; matrix products, arithmetic and copies ran while one was open for 0% of the time, Pallas kernels for 15%

profile of v2, /device:TPU:0, one launch (start us, length us, event | category | flops | bytes accessed | tf_op | source)
XLA Modules:
  0.0 68.8 jit_solution(7139651875503471586)
XLA Ops:
  0.6 0.0 copy-start
  0.6 1.7 %copy-done = f32[3,27,8,8,128]{4,3,2,1,0:T(8,128)S(1)} copy-done((f32[3,27,8,8,128]{4,3,2,1,0:T(8,128)S(1)}, f32[3,27,8,8,128]{4,3,2,1,0:T(8,128)}, u32[]{:S(2)}) %copy-start) | copy-done | bytes 2654232
  2.4 0.0 copy-start.2
  2.4 1.2 %copy-done.2 = f32[27,8,8,128]{3,2,1,0:T(8,128)S(1)} copy-done((f32[27,8,8,128]{3,2,1,0:T(8,128)S(1)}, f32[27,8,8,128]{3,2,1,0:T(8,128)}, u32[]{:S(2)}) %copy-start.2) | copy-done | bytes 884760
  3.6 0.8 %copy-done.3 = s32[8,8,128]{2,1,0:T(8,128)S(1)} copy-done((s32[8,8,128]{2,1,0:T(8,128)S(1)}, s32[8,8,128]{2,1,0:T(8,128)}, u32[]{:S(2)}) %copy-start.3) | copy-done | bytes 32792
  4.3 0.8 %copy-done.5 = f32[8,8,128]{2,1,0:T(8,128)S(1)} copy-done((f32[8,8,128]{2,1,0:T(8,128)S(1)}, f32[8,8,128]{2,1,0:T(8,128)}, u32[]{:S(2)}) %copy-start.5) | copy-done | bytes 32792
  5.1 0.8 %open.1 = (f32[72,128]{1,0:T(8,128)S(1)}, f32[72,128]{1,0:T(8,128)S(1)}, f32[520,128]{1,0:T(8,128)S(1)}, f32[520,128]{1,0:T(8,128)S(1)}, f32[576,128]{1,0:T(8,128)S(1)}) custom-call(f32[1728,128]{1,0:T(8,128)S(1)} %bitcast.10, f32[5184,128]{1,0:T(8,128)S(1)} %bitcast.6, f32[64,128]{1,0:T(8,128)S(1)} %bitcast.16, s32[64,128]{1,0:T(8,128)S(1)} %bitcast.12), custom_call_target="tpu_custom_call" | custom-call | flops 1638400 | bytes 4505600 | tf_op jit(solution)/shard_map/open/pallas_call | solution.py:440
  5.8 3.1 %collective-permute-start.2 = (f32[520,128]{1,0:T(8,128)S(1)}, f32[520,128]{1,0:T(8,128)S(1)}, u32[]{:S(2)}, u32[]{:S(2)}) collective-permute-start(f32[520,128]{1,0:T(8,128)S(1)} %get-tuple-element.27), channel_id=1, source_target_pairs={{0,8},{1,9},{2,10},{3,11},{8,0},{9,1},{10,2},{11,3},{16,24},{17,25... | collective-permute-start | bytes 798728 | tf_op jit(solution)/shard_map/ppermute | solution.py:55
  8.9 0.0 collective-permute-start.3
  8.9 0.5 collective-permute-start
  9.4 1.1 %collective-permute-start.1 = (f32[72,128]{1,0:T(8,128)S(1)}, f32[72,128]{1,0:T(8,128)S(1)}, u32[]{:S(2)}, u32[]{:S(2)}) collective-permute-start(f32[72,128]{1,0:T(8,128)S(1)} %get-tuple-element.24), channel_id=1, source_target_pairs={{0,3},{1,2},{2,1},{3,0},{4,7},{5,6},{6,5},{7,4},{8,11},{9,10},{10,... | collective-permute-start | bytes 110600 | tf_op jit(solution)/shard_map/ppermute | solution.py:55
  10.5 0.0 collective-permute-done.za
  10.5 2.5 %collective-permute-done.1.zb = f32[72,128]{1,0:T(8,128)S(1)} collective-permute-done((f32[72,128]{1,0:T(8,128)S(1)}, f32[72,128]{1,0:T(8,128)S(1)}, u32[]{:S(2)}, u32[]{:S(2)}) %collective-permute-start.1) | collective-permute-done | bytes 36896 | tf_op jit(solution)/shard_map/ppermute | solution.py:55
  13.0 10.4 %second.1 = (f32[56,128]{1,0:T(8,128)S(1)}, f32[56,128]{1,0:T(8,128)S(1)}, f32[3456,128]{1,0:T(8,128)S(1)}, f32[1024,128]{1,0:T(8,128)S(1)}) custom-call(f32[1728,128]{1,0:T(8,128)S(1)} %bitcast.11, f32[576,128]{1,0:T(8,128)S(1)} %get-tuple-element.22.mom, f32[72,128]{1,0:T(8,128)S(1)} %collective-permute-done.za, f32[72,128]{1,0:T(8,128)S(1)} %collective-permute-done.1.zb), custom_call_target="tpu_custom_call" | custom-call | flops 819200 | bytes 3604480 | tf_op jit(solution)/shard_map/second/pallas_call | solution.py:440
  23.4 2.5 %collective-permute-start.4 = (f32[56,128]{1,0:T(8,128)S(1)}, f32[56,128]{1,0:T(8,128)S(1)}, u32[]{:S(2)}, u32[]{:S(2)}) collective-permute-start(f32[56,128]{1,0:T(8,128)S(1)} %get-tuple-element.29), channel_id=1, source_target_pairs={{0,8},{1,9},{2,10},{3,11},{8,0},{9,1},{10,2},{11,3},{16,24},{17,25... | collective-permute-start | bytes 86024 | tf_op jit(solution)/shard_map/ppermute | solution.py:55
  25.9 0.5 collective-permute-start.5
  26.4 1.5 %collective-permute-done.4.sa = f32[56,128]{1,0:T(8,128)S(1)} collective-permute-done((f32[56,128]{1,0:T(8,128)S(1)}, f32[56,128]{1,0:T(8,128)S(1)}, u32[]{:S(2)}, u32[]{:S(2)}) %collective-permute-start.4) | collective-permute-done | bytes 28704 | tf_op jit(solution)/shard_map/ppermute | solution.py:55
  27.9 0.0 collective-permute-done.5.sb
  27.9 0.0 collective-permute-done.2.xa
  27.9 0.0 collective-permute-done.3.xb
  27.9 1.2 %third.1 = (f32[3456,128]{1,0:T(8,128)S(1)}, f32[1024,128]{1,0:T(8,128)S(1)}, f32[144,128]{1,0:T(8,128)S(1)}, f32[144,128]{1,0:T(8,128)}) custom-call(f32[3456,128]{1,0:T(8,128)S(1)} %get-tuple-element.25.field, f32[1024,128]{1,0:T(8,128)S(1)} %get-tuple-element.26.extra, ...), custom_call_target="tpu_custom_call", output_to_operand_aliasing={{0}: (0, {}), {1}: (1, {})} | custom-call | flops 819200 | bytes 5324800 | tf_op jit(solution)/shard_map/third/pallas_call | solution.py:440
  29.1 1.5 %collective-permute-start.6 = (f32[144,128]{1,0:T(8,128)S(1)}, f32[144,128]{1,0:T(8,128)S(1)}, u32[]{:S(2)}, u32[]{:S(2)}) collective-permute-start(f32[144,128]{1,0:T(8,128)S(1)} %get-tuple-element.33), channel_id=1, source_target_pairs={{0,4},{1,5},{2,6},{3,7},{4,0},{5,1},{6,2},{7,3},{8,12},{9,13},{10,... | collective-permute-start | bytes 221192 | tf_op jit(solution)/shard_map/ppermute | solution.py:55
  30.6 2.8 %collective-permute-done.6.ya.yb = f32[144,128]{1,0:T(8,128)S(1)} collective-permute-done((f32[144,128]{1,0:T(8,128)S(1)}, f32[144,128]{1,0:T(8,128)S(1)}, u32[]{:S(2)}, u32[]{:S(2)}) %collective-permute-start.6) | collective-permute-done | bytes 73760 | tf_op jit(solution)/shard_map/ppermute | solution.py:55
  33.4 0.0 copy-done.1
  33.5 0.0 copy-done.4
  33.5 12.4 %step2.1 = (f32[3456,128]{1,0:T(8,128)S(1)}, f32[3456,128]{1,0:T(8,128)S(1)}, f32[64,128]{1,0:T(8,128)S(1)}, f32[144,128]{1,0:T(8,128)S(1)}, f32[144,128]{1,0:T(8,128)}) custom-call(f32[3456,128]{1,0:T(8,128)S(1)} %get-tuple-element.31.field, f32[1024,128]{1,0:T(8,128)S(1)} %get-tuple-element.32.extra, ...), custom_call_target="tpu_custom_call", output_to_operand_aliasing={{0}: (0, {})} | custom-call | flops 3276800 | bytes 9175040 | tf_op jit(solution)/shard_map/step2/pallas_call | solution.py:440
  45.9 1.5 %collective-permute-start.7 = (f32[144,128]{1,0:T(8,128)S(1)}, f32[144,128]{1,0:T(8,128)S(1)}, u32[]{:S(2)}, u32[]{:S(2)}) collective-permute-start(f32[144,128]{1,0:T(8,128)S(1)} %get-tuple-element.35), channel_id=1, source_target_pairs={{0,4},{1,5},{2,6},{3,7},{4,0},{5,1},{6,2},{7,3},{8,12},{9,13},{10,... | collective-permute-start | bytes 221192 | tf_op jit(solution)/shard_map/ppermute | solution.py:55
  47.4 2.8 %collective-permute-done.7.ya.yb = f32[144,128]{1,0:T(8,128)S(1)} collective-permute-done((f32[144,128]{1,0:T(8,128)S(1)}, f32[144,128]{1,0:T(8,128)S(1)}, u32[]{:S(2)}, u32[]{:S(2)}) %collective-permute-start.7) | collective-permute-done | bytes 73760 | tf_op jit(solution)/shard_map/ppermute | solution.py:55
  50.2 12.2 %step1.1 = (f32[3456,128]{1,0:T(8,128)S(1)}, f32[3456,128]{1,0:T(8,128)S(1)}, f32[64,128]{1,0:T(8,128)S(1)}, f32[144,128]{1,0:T(8,128)S(1)}, f32[144,128]{1,0:T(8,128)}) custom-call(f32[3456,128]{1,0:T(8,128)S(1)} %get-tuple-element.34.field, f32[1024,128]{1,0:T(8,128)S(1)} %get-tuple-element.32.extra, ...), custom_call_target="tpu_custom_call", output_to_operand_aliasing={{0}: (0, {})} | custom-call | flops 3276800 | bytes 9175040 | tf_op jit(solution)/shard_map/step1/pallas_call | solution.py:440
  62.4 1.5 %collective-permute-start.8 = (f32[144,128]{1,0:T(8,128)S(1)}, f32[144,128]{1,0:T(8,128)S(1)}, u32[]{:S(2)}, u32[]{:S(2)}) collective-permute-start(f32[144,128]{1,0:T(8,128)S(1)} %get-tuple-element.38), channel_id=1, source_target_pairs={{0,4},{1,5},{2,6},{3,7},{4,0},{5,1},{6,2},{7,3},{8,12},{9,13},{10,... | collective-permute-start | bytes 221192 | tf_op jit(solution)/shard_map/ppermute | solution.py:55
  63.9 2.8 %collective-permute-done.8.ya.yb = f32[144,128]{1,0:T(8,128)S(1)} collective-permute-done((f32[144,128]{1,0:T(8,128)S(1)}, f32[144,128]{1,0:T(8,128)S(1)}, u32[]{:S(2)}, u32[]{:S(2)}) %collective-permute-start.8) | collective-permute-done | bytes 73760 | tf_op jit(solution)/shard_map/ppermute | solution.py:55
  66.8 2.0 %step0.1 = (f32[3456,128]{1,0:T(8,128)S(1)}, f32[1728,128]{1,0:T(8,128)}, f32[64,128]{1,0:T(8,128)}) custom-call(f32[3456,128]{1,0:T(8,128)S(1)} %get-tuple-element.37.field, f32[1024,128]{1,0:T(8,128)S(1)} %get-tuple-element.32.extra, f32[576,128]{1,0:T(8,128)S(1)} %get-tuple-element.22.mom, ...), custom_call_target="tpu_custom_call", output_to_operand_aliasing={{0}: (0, {})} | custom-call | flops 3276800 | bytes 8142848 | tf_op jit(solution)/shard_map/step0/pallas_call | solution.py:440
  (5 shorter events, 0.0 us)
Async XLA Ops:
  0.6 1.8 %copy-start = (f32[3,27,8,8,128]{4,3,2,1,0:T(8,128)S(1)}, f32[3,27,8,8,128]{4,3,2,1,0:T(8,128)}, u32[]{:S(2)}) copy-start(f32[3,27,8,8,128]{4,3,2,1,0:T(8,128)} %param.4) | copy-start | bytes 7962628
  2.4 1.2 %copy-start.2 = (f32[27,8,8,128]{3,2,1,0:T(8,128)S(1)}, f32[27,8,8,128]{3,2,1,0:T(8,128)}, u32[]{:S(2)}) copy-start(f32[27,8,8,128]{3,2,1,0:T(8,128)} %param.7) | copy-start | bytes 2654212
  3.6 0.8 %copy-start.3 = (s32[8,8,128]{2,1,0:T(8,128)S(1)}, s32[8,8,128]{2,1,0:T(8,128)}, u32[]{:S(2)}) copy-start(s32[8,8,128]{2,1,0:T(8,128)} %param.6) | copy-start | bytes 98308
  4.3 0.8 %copy-start.5 = (f32[8,8,128]{2,1,0:T(8,128)S(1)}, f32[8,8,128]{2,1,0:T(8,128)}, u32[]{:S(2)}) copy-start(f32[8,8,128]{2,1,0:T(8,128)} %param.5) | copy-start | bytes 98308
  5.8 22.1 %collective-permute-start.2 = (f32[520,128]{1,0:T(8,128)S(1)}, f32[520,128]{1,0:T(8,128)S(1)}, u32[]{:S(2)}, u32[]{:S(2)}) collective-permute-start(f32[520,128]{1,0:T(8,128)S(1)} %get-tuple-element.27), channel_id=1, source_target_pairs={{0,8},{1,9},{2,10},{3,11},{8,0},{9,1},{10,2},{11,3},{16,24},{17,25... | collective-permute-start | bytes 798728 | tf_op jit(solution)/shard_map/ppermute | solution.py:55
  8.9 19.0 %collective-permute-start.3 = (f32[520,128]{1,0:T(8,128)S(1)}, f32[520,128]{1,0:T(8,128)S(1)}, u32[]{:S(2)}, u32[]{:S(2)}) collective-permute-start(f32[520,128]{1,0:T(8,128)S(1)} %get-tuple-element.28), channel_id=1, source_target_pairs={{0,1},{1,0},{2,3},{3,2},{8,16},{9,17},{10,18},{11,19},{16,8},{17,9... | collective-permute-start | bytes 798728 | tf_op jit(solution)/shard_map/ppermute | solution.py:55
  8.9 1.6 %collective-permute-start = (f32[72,128]{1,0:T(8,128)S(1)}, f32[72,128]{1,0:T(8,128)S(1)}, u32[]{:S(2)}, u32[]{:S(2)}) collective-permute-start(f32[72,128]{1,0:T(8,128)S(1)} %get-tuple-element.23), channel_id=1, source_target_pairs={{0,1},{1,0},{2,3},{3,2},{4,5},{5,4},{6,7},{7,6},{8,9},{9,8},{10,11... | collective-permute-start | bytes 110600 | tf_op jit(solution)/shard_map/ppermute | solution.py:55
  9.4 3.6 %collective-permute-start.1 = (f32[72,128]{1,0:T(8,128)S(1)}, f32[72,128]{1,0:T(8,128)S(1)}, u32[]{:S(2)}, u32[]{:S(2)}) collective-permute-start(f32[72,128]{1,0:T(8,128)S(1)} %get-tuple-element.24), channel_id=1, source_target_pairs={{0,3},{1,2},{2,1},{3,0},{4,7},{5,6},{6,5},{7,4},{8,11},{9,10},{10,... | collective-permute-start | bytes 110600 | tf_op jit(solution)/shard_map/ppermute | solution.py:55
  23.4 10.0 %copy-start.1 = (f32[3,27,8,8,128]{4,3,2,1,0:T(8,128)S(1)}, f32[3,27,8,8,128]{4,3,2,1,0:T(8,128)}, u32[]{:S(2)}) copy-start(f32[3,27,8,8,128]{4,3,2,1,0:T(8,128)} %param.4) | copy-start | bytes 7962628
  23.4 10.0 %copy-start.4 = (s32[8,8,128]{2,1,0:T(8,128)S(1)}, s32[8,8,128]{2,1,0:T(8,128)}, u32[]{:S(2)}) copy-start(s32[8,8,128]{2,1,0:T(8,128)} %param.6) | copy-start | bytes 98308
  23.4 4.5 %collective-permute-start.4 = (f32[56,128]{1,0:T(8,128)S(1)}, f32[56,128]{1,0:T(8,128)S(1)}, u32[]{:S(2)}, u32[]{:S(2)}) collective-permute-start(f32[56,128]{1,0:T(8,128)S(1)} %get-tuple-element.29), channel_id=1, source_target_pairs={{0,8},{1,9},{2,10},{3,11},{8,0},{9,1},{10,2},{11,3},{16,24},{17,25... | collective-permute-start | bytes 86024 | tf_op jit(solution)/shard_map/ppermute | solution.py:55
  25.9 2.0 %collective-permute-start.5 = (f32[56,128]{1,0:T(8,128)S(1)}, f32[56,128]{1,0:T(8,128)S(1)}, u32[]{:S(2)}, u32[]{:S(2)}) collective-permute-start(f32[56,128]{1,0:T(8,128)S(1)} %get-tuple-element.30), channel_id=1, source_target_pairs={{0,1},{1,0},{2,3},{3,2},{8,16},{9,17},{10,18},{11,19},{16,8},{17,9... | collective-permute-start | bytes 86024 | tf_op jit(solution)/shard_map/ppermute | solution.py:55
  29.1 4.4 %collective-permute-start.6 = (f32[144,128]{1,0:T(8,128)S(1)}, f32[144,128]{1,0:T(8,128)S(1)}, u32[]{:S(2)}, u32[]{:S(2)}) collective-permute-start(f32[144,128]{1,0:T(8,128)S(1)} %get-tuple-element.33), channel_id=1, source_target_pairs={{0,4},{1,5},{2,6},{3,7},{4,0},{5,1},{6,2},{7,3},{8,12},{9,13},{10,... | collective-permute-start | bytes 221192 | tf_op jit(solution)/shard_map/ppermute | solution.py:55
  45.9 4.4 %collective-permute-start.7 = (f32[144,128]{1,0:T(8,128)S(1)}, f32[144,128]{1,0:T(8,128)S(1)}, u32[]{:S(2)}, u32[]{:S(2)}) collective-permute-start(f32[144,128]{1,0:T(8,128)S(1)} %get-tuple-element.35), channel_id=1, source_target_pairs={{0,4},{1,5},{2,6},{3,7},{4,0},{5,1},{6,2},{7,3},{8,12},{9,13},{10,... | collective-permute-start | bytes 221192 | tf_op jit(solution)/shard_map/ppermute | solution.py:55
  62.4 4.4 %collective-permute-start.8 = (f32[144,128]{1,0:T(8,128)S(1)}, f32[144,128]{1,0:T(8,128)S(1)}, u32[]{:S(2)}, u32[]{:S(2)}) collective-permute-start(f32[144,128]{1,0:T(8,128)S(1)} %get-tuple-element.38), channel_id=1, source_target_pairs={{0,4},{1,5},{2,6},{3,7},{4,0},{5,1},{6,2},{7,3},{8,12},{9,13},{10,... | collective-permute-start | bytes 221192 | tf_op jit(solution)/shard_map/ppermute | solution.py:55

commit v3 on v2

--- a/solution.py
+++ b/solution.py
@@ -156,7 +156,7 @@
     def source(q, x):
         if q < Q:
             return seed[g.raw(q, x), :]
-        return mom[g.raw({U2: 1, U1: 5, SOLID: 8}[q - q % 3 if q < SOLID else q] + (q % 3 if q < SOLID else 0), x), :]
+        return mom[g.raw({0: 1, 1: 5, 2: 8}[(q - Q) // 3] + (q - Q) % 3, x), :]
 
     lane = lanes(g)
     group, offset = lane // SLOTS, lane % SLOTS
@@ -232,7 +232,7 @@
             down = jnp.where(part, roll(tile, j * width - DEPTH * SLOTS, 1), down)
         sa[g.tile(k), :], sb[g.tile(k), :] = x.send(up, down)
 
-    def row(r, carry):
+    for r in range(nx):
         for i in range(Q):
             field[g.at(i, r + DEPTH), :] = seed[g.raw(i, r), :]
             swap_edges(g, field, i, r + DEPTH)
@@ -242,9 +242,6 @@
         solid = mom[g.raw(8, r), :]
         extra[g.at(6, r + DEPTH), :] = solid
         extra[g.at(7, r + DEPTH), :] = 1.0 - solid
-        return carry
-
-    lax.fori_loop(0, nx, row, 0)
 
 
 def y_message(g, field, ya, yb):
@@ -401,7 +398,7 @@
 
     def inner(x, carry):
         row = x + DEPTH
-        here = pl.ds(pl.multiple_of(x * g.ny, g.ny), g.ny)
+        here = g.tile(x) if step else pl.ds(pl.multiple_of(x * g.ny, g.ny), g.ny)
         p = pull(row)
         if step:
             u, solid, fluidity = parts(row)
@@ -424,14 +421,13 @@
                 result[g.raw(i, x), :] = out[i]
         return carry
 
-    lax.fori_loop(0, nx, inner, 0)
-    if step:
-        for r in range(DEPTH - step + 1 - 1, DEPTH):
-            if r >= STEPS - step:
-                outer(r)
-        for r in range(DEPTH + nx, DEPTH + nx + step):
-            if r < DEPTH + nx + step - 0:
-                outer(r)
+    if not step:
+        lax.fori_loop(0, nx, inner, 0)
+    else:
+        for x in range(nx):
+            inner(x, 0)
+        for r in (*range(DEPTH - step, DEPTH), *range(DEPTH + nx, DEPTH + nx + step)):
+            outer(r)
         y_message(g, result, *messages)
 
 

time: 69.1 us -> 39.2 us (0.57)
  Pallas kernels: 38.9 us -> 8.99 us
    pallas_call x6, Pallas kernels: 38.9 us -> 8.99 us  [call(): pl.pallas_call(kernel, name=name, out_shape=[jax.ShapeDtypeStruct(o, jnp....]
  transfers between devices with their start and end apart: 9 -> 9, of which waited for: 5 -> 5; matrix products, arithmetic and copies ran while one was open for 0% -> 0% of each run, Pallas kernels for 15% -> 1%
where the time goes in v3:
time: 39.2 us; the launch traced here: 38.9 us
  waiting for transfers between devices  12.5 us (32%)
  starting transfers between devices  12.3 us (31%)
  Pallas kernels  8.99 us (23%)
  local copies, waits for them, and re-layouts  4.44 us (11%)
  between operations  0.68 us (2%)
    ppermute x9, waiting for transfers between devices, swapped(): return lax.ppermute(value, (axis, spare) if spare else axis, pairs)  12.5 us
    ppermute x9, starting transfers between devices, swapped(): return lax.ppermute(value, (axis, spare) if spare else axis, pairs)  12.3 us
    pallas_call x6, Pallas kernels, call(): pl.pallas_call(kernel, name=name, out_shape=[jax.ShapeDtypeStruct(o, jnp....  8.99 us
    unnamed x12, local copies, waits for them, and re-layouts  4.44 us
  transfers between devices with their start and end apart: 9, of which 5 were waited for; matrix products, arithmetic and copies ran while one was open for 0% of the time, Pallas kernels for 1%

profile of v3, /device:TPU:0, one launch (start us, length us, event | category | flops | bytes accessed | tf_op | source)
XLA Modules:
  0.0 38.9 jit_solution(2603011777399544296)
XLA Ops:
  0.6 0.0 copy-start
  0.6 1.7 %copy-done = f32[3,27,8,8,128]{4,3,2,1,0:T(8,128)S(1)} copy-done((f32[3,27,8,8,128]{4,3,2,1,0:T(8,128)S(1)}, f32[3,27,8,8,128]{4,3,2,1,0:T(8,128)}, u32[]{:S(2)}) %copy-start) | copy-done | bytes 2654232
  2.4 1.2 %copy-done.2 = f32[27,8,8,128]{3,2,1,0:T(8,128)S(1)} copy-done((f32[27,8,8,128]{3,2,1,0:T(8,128)S(1)}, f32[27,8,8,128]{3,2,1,0:T(8,128)}, u32[]{:S(2)}) %copy-start.2) | copy-done | bytes 884760
  3.6 0.8 %copy-done.3 = s32[8,8,128]{2,1,0:T(8,128)S(1)} copy-done((s32[8,8,128]{2,1,0:T(8,128)S(1)}, s32[8,8,128]{2,1,0:T(8,128)}, u32[]{:S(2)}) %copy-start.3) | copy-done | bytes 32792
  4.3 0.8 %copy-done.5 = f32[8,8,128]{2,1,0:T(8,128)S(1)} copy-done((f32[8,8,128]{2,1,0:T(8,128)S(1)}, f32[8,8,128]{2,1,0:T(8,128)}, u32[]{:S(2)}) %copy-start.5) | copy-done | bytes 32792
  5.1 0.8 %open.1 = (f32[72,128]{1,0:T(8,128)S(1)}, f32[72,128]{1,0:T(8,128)S(1)}, f32[520,128]{1,0:T(8,128)S(1)}, f32[520,128]{1,0:T(8,128)S(1)}, f32[576,128]{1,0:T(8,128)S(1)}) custom-call(f32[1728,128]{1,0:T(8,128)S(1)} %bitcast.10, f32[5184,128]{1,0:T(8,128)S(1)} %bitcast.6, f32[64,128]{1,0:T(8,128)S(1)} %bitcast.16, s32[64,128]{1,0:T(8,128)S(1)} %bitcast.12), custom_call_target="tpu_custom_call" | custom-call | flops 1638400 | bytes 4505600 | tf_op jit(solution)/shard_map/open/pallas_call | solution.py:436
  5.8 3.1 %collective-permute-start.2 = (f32[520,128]{1,0:T(8,128)S(1)}, f32[520,128]{1,0:T(8,128)S(1)}, u32[]{:S(2)}, u32[]{:S(2)}) collective-permute-start(f32[520,128]{1,0:T(8,128)S(1)} %get-tuple-element.27), channel_id=1, source_target_pairs={{0,8},{1,9},{2,10},{3,11},{8,0},{9,1},{10,2},{11,3},{16,24},{17,25... | collective-permute-start | bytes 798728 | tf_op jit(solution)/shard_map/ppermute | solution.py:55
  8.9 0.0 collective-permute-start.3
  8.9 0.5 %collective-permute-start = (f32[72,128]{1,0:T(8,128)S(1)}, f32[72,128]{1,0:T(8,128)S(1)}, u32[]{:S(2)}, u32[]{:S(2)}) collective-permute-start(f32[72,128]{1,0:T(8,128)S(1)} %get-tuple-element.23), channel_id=1, source_target_pairs={{0,1},{1,0},{2,3},{3,2},{4,5},{5,4},{6,7},{7,6},{8,9},{9,8},{10,11... | collective-permute-start | bytes 110600 | tf_op jit(solution)/shard_map/ppermute | solution.py:55
  9.4 1.1 %collective-permute-start.1 = (f32[72,128]{1,0:T(8,128)S(1)}, f32[72,128]{1,0:T(8,128)S(1)}, u32[]{:S(2)}, u32[]{:S(2)}) collective-permute-start(f32[72,128]{1,0:T(8,128)S(1)} %get-tuple-element.24), channel_id=1, source_target_pairs={{0,3},{1,2},{2,1},{3,0},{4,7},{5,6},{6,5},{7,4},{8,11},{9,10},{10,... | collective-permute-start | bytes 110600 | tf_op jit(solution)/shard_map/ppermute | solution.py:55
  10.5 0.0 collective-permute-done.za
  10.5 2.5 %collective-permute-done.1.zb = f32[72,128]{1,0:T(8,128)S(1)} collective-permute-done((f32[72,128]{1,0:T(8,128)S(1)}, f32[72,128]{1,0:T(8,128)S(1)}, u32[]{:S(2)}, u32[]{:S(2)}) %collective-permute-start.1) | collective-permute-done | bytes 36896 | tf_op jit(solution)/shard_map/ppermute | solution.py:55
  13.0 0.6 %second.1 = (f32[56,128]{1,0:T(8,128)S(1)}, f32[56,128]{1,0:T(8,128)S(1)}, f32[3456,128]{1,0:T(8,128)S(1)}, f32[1024,128]{1,0:T(8,128)S(1)}) custom-call(f32[1728,128]{1,0:T(8,128)S(1)} %bitcast.11, f32[576,128]{1,0:T(8,128)S(1)} %get-tuple-element.22.mom, f32[72,128]{1,0:T(8,128)S(1)} %collective-permute-done.za, f32[72,128]{1,0:T(8,128)S(1)} %collective-permute-done.1.zb), custom_call_target="tpu_custom_call" | custom-call | flops 819200 | bytes 3604480 | tf_op jit(solution)/shard_map/second/pallas_call | solution.py:436
  13.6 0.0 copy-start.1
  13.6 0.0 copy-start.4
  13.6 2.5 %collective-permute-start.4 = (f32[56,128]{1,0:T(8,128)S(1)}, f32[56,128]{1,0:T(8,128)S(1)}, u32[]{:S(2)}, u32[]{:S(2)}) collective-permute-start(f32[56,128]{1,0:T(8,128)S(1)} %get-tuple-element.29), channel_id=1, source_target_pairs={{0,8},{1,9},{2,10},{3,11},{8,0},{9,1},{10,2},{11,3},{16,24},{17,25... | collective-permute-start | bytes 86024 | tf_op jit(solution)/shard_map/ppermute | solution.py:55
  16.1 0.5 %collective-permute-start.5 = (f32[56,128]{1,0:T(8,128)S(1)}, f32[56,128]{1,0:T(8,128)S(1)}, u32[]{:S(2)}, u32[]{:S(2)}) collective-permute-start(f32[56,128]{1,0:T(8,128)S(1)} %get-tuple-element.30), channel_id=1, source_target_pairs={{0,1},{1,0},{2,3},{3,2},{8,16},{9,17},{10,18},{11,19},{16,8},{17,9... | collective-permute-start | bytes 86024 | tf_op jit(solution)/shard_map/ppermute | solution.py:55
  16.6 1.5 %collective-permute-done.4.sa = f32[56,128]{1,0:T(8,128)S(1)} collective-permute-done((f32[56,128]{1,0:T(8,128)S(1)}, f32[56,128]{1,0:T(8,128)S(1)}, u32[]{:S(2)}, u32[]{:S(2)}) %collective-permute-start.4) | collective-permute-done | bytes 28704 | tf_op jit(solution)/shard_map/ppermute | solution.py:55
  18.2 0.0 collective-permute-done.5.sb
  18.2 0.0 collective-permute-done.2.xa
  18.2 0.0 collective-permute-done.3.xb
  18.2 1.2 %third.1 = (f32[3456,128]{1,0:T(8,128)S(1)}, f32[1024,128]{1,0:T(8,128)S(1)}, f32[144,128]{1,0:T(8,128)S(1)}, f32[144,128]{1,0:T(8,128)}) custom-call(f32[3456,128]{1,0:T(8,128)S(1)} %get-tuple-element.25.field, f32[1024,128]{1,0:T(8,128)S(1)} %get-tuple-element.26.extra, ...), custom_call_target="tpu_custom_call", output_to_operand_aliasing={{0}: (0, {}), {1}: (1, {})} | custom-call | flops 819200 | bytes 5324800 | tf_op jit(solution)/shard_map/third/pallas_call | solution.py:436
  19.3 1.5 %collective-permute-start.6 = (f32[144,128]{1,0:T(8,128)S(1)}, f32[144,128]{1,0:T(8,128)S(1)}, u32[]{:S(2)}, u32[]{:S(2)}) collective-permute-start(f32[144,128]{1,0:T(8,128)S(1)} %get-tuple-element.33), channel_id=1, source_target_pairs={{0,4},{1,5},{2,6},{3,7},{4,0},{5,1},{6,2},{7,3},{8,12},{9,13},{10,... | collective-permute-start | bytes 221192 | tf_op jit(solution)/shard_map/ppermute | solution.py:55
  20.9 2.8 %collective-permute-done.6.ya.yb = f32[144,128]{1,0:T(8,128)S(1)} collective-permute-done((f32[144,128]{1,0:T(8,128)S(1)}, f32[144,128]{1,0:T(8,128)S(1)}, u32[]{:S(2)}, u32[]{:S(2)}) %collective-permute-start.6) | collective-permute-done | bytes 73760 | tf_op jit(solution)/shard_map/ppermute | solution.py:55
  23.7 0.0 copy-done.1
  23.7 2.4 %step2.1 = (f32[3456,128]{1,0:T(8,128)S(1)}, f32[3456,128]{1,0:T(8,128)S(1)}, f32[64,128]{1,0:T(8,128)S(1)}, f32[144,128]{1,0:T(8,128)S(1)}, f32[144,128]{1,0:T(8,128)}) custom-call(f32[3456,128]{1,0:T(8,128)S(1)} %get-tuple-element.31.field, f32[1024,128]{1,0:T(8,128)S(1)} %get-tuple-element.32.extra, ...), custom_call_target="tpu_custom_call", output_to_operand_aliasing={{0}: (0, {})} | custom-call | flops 3276800 | bytes 9175040 | tf_op jit(solution)/shard_map/step2/pallas_call | solution.py:436
  26.1 1.5 %collective-permute-start.7 = (f32[144,128]{1,0:T(8,128)S(1)}, f32[144,128]{1,0:T(8,128)S(1)}, u32[]{:S(2)}, u32[]{:S(2)}) collective-permute-start(f32[144,128]{1,0:T(8,128)S(1)} %get-tuple-element.35), channel_id=1, source_target_pairs={{0,4},{1,5},{2,6},{3,7},{4,0},{5,1},{6,2},{7,3},{8,12},{9,13},{10,... | collective-permute-start | bytes 221192 | tf_op jit(solution)/shard_map/ppermute | solution.py:55
  27.6 2.8 %collective-permute-done.7.ya.yb = f32[144,128]{1,0:T(8,128)S(1)} collective-permute-done((f32[144,128]{1,0:T(8,128)S(1)}, f32[144,128]{1,0:T(8,128)S(1)}, u32[]{:S(2)}, u32[]{:S(2)}) %collective-permute-start.7) | collective-permute-done | bytes 73760 | tf_op jit(solution)/shard_map/ppermute | solution.py:55
  30.4 2.1 %step1.1 = (f32[3456,128]{1,0:T(8,128)S(1)}, f32[3456,128]{1,0:T(8,128)S(1)}, f32[64,128]{1,0:T(8,128)S(1)}, f32[144,128]{1,0:T(8,128)S(1)}, f32[144,128]{1,0:T(8,128)}) custom-call(f32[3456,128]{1,0:T(8,128)S(1)} %get-tuple-element.34.field, f32[1024,128]{1,0:T(8,128)S(1)} %get-tuple-element.32.extra, ...), custom_call_target="tpu_custom_call", output_to_operand_aliasing={{0}: (0, {})} | custom-call | flops 3276800 | bytes 9175040 | tf_op jit(solution)/shard_map/step1/pallas_call | solution.py:436
  32.5 1.5 %collective-permute-start.8 = (f32[144,128]{1,0:T(8,128)S(1)}, f32[144,128]{1,0:T(8,128)S(1)}, u32[]{:S(2)}, u32[]{:S(2)}) collective-permute-start(f32[144,128]{1,0:T(8,128)S(1)} %get-tuple-element.38), channel_id=1, source_target_pairs={{0,4},{1,5},{2,6},{3,7},{4,0},{5,1},{6,2},{7,3},{8,12},{9,13},{10,... | collective-permute-start | bytes 221192 | tf_op jit(solution)/shard_map/ppermute | solution.py:55
  34.1 2.8 %collective-permute-done.8.ya.yb = f32[144,128]{1,0:T(8,128)S(1)} collective-permute-done((f32[144,128]{1,0:T(8,128)S(1)}, f32[144,128]{1,0:T(8,128)S(1)}, u32[]{:S(2)}, u32[]{:S(2)}) %collective-permute-start.8) | collective-permute-done | bytes 73760 | tf_op jit(solution)/shard_map/ppermute | solution.py:55
  36.9 2.0 %step0.1 = (f32[3456,128]{1,0:T(8,128)S(1)}, f32[1728,128]{1,0:T(8,128)}, f32[64,128]{1,0:T(8,128)}) custom-call(f32[3456,128]{1,0:T(8,128)S(1)} %get-tuple-element.37.field, f32[1024,128]{1,0:T(8,128)S(1)} %get-tuple-element.32.extra, f32[576,128]{1,0:T(8,128)S(1)} %get-tuple-element.22.mom, ...), custom_call_target="tpu_custom_call", output_to_operand_aliasing={{0}: (0, {})} | custom-call | flops 3276800 | bytes 8142848 | tf_op jit(solution)/shard_map/step0/pallas_call | solution.py:436
  (5 shorter events, 0.0 us)
Async XLA Ops:
  0.6 1.8 %copy-start = (f32[3,27,8,8,128]{4,3,2,1,0:T(8,128)S(1)}, f32[3,27,8,8,128]{4,3,2,1,0:T(8,128)}, u32[]{:S(2)}) copy-start(f32[3,27,8,8,128]{4,3,2,1,0:T(8,128)} %param.4) | copy-start | bytes 7962628
  2.4 1.2 %copy-start.2 = (f32[27,8,8,128]{3,2,1,0:T(8,128)S(1)}, f32[27,8,8,128]{3,2,1,0:T(8,128)}, u32[]{:S(2)}) copy-start(f32[27,8,8,128]{3,2,1,0:T(8,128)} %param.7) | copy-start | bytes 2654212
  3.6 0.8 %copy-start.3 = (s32[8,8,128]{2,1,0:T(8,128)S(1)}, s32[8,8,128]{2,1,0:T(8,128)}, u32[]{:S(2)}) copy-start(s32[8,8,128]{2,1,0:T(8,128)} %param.6) | copy-start | bytes 98308
  4.3 0.8 %copy-start.5 = (f32[8,8,128]{2,1,0:T(8,128)S(1)}, f32[8,8,128]{2,1,0:T(8,128)}, u32[]{:S(2)}) copy-start(f32[8,8,128]{2,1,0:T(8,128)} %param.5) | copy-start | bytes 98308
  5.8 12.3 %collective-permute-start.2 = (f32[520,128]{1,0:T(8,128)S(1)}, f32[520,128]{1,0:T(8,128)S(1)}, u32[]{:S(2)}, u32[]{:S(2)}) collective-permute-start(f32[520,128]{1,0:T(8,128)S(1)} %get-tuple-element.27), channel_id=1, source_target_pairs={{0,8},{1,9},{2,10},{3,11},{8,0},{9,1},{10,2},{11,3},{16,24},{17,25... | collective-permute-start | bytes 798728 | tf_op jit(solution)/shard_map/ppermute | solution.py:55
  8.9 9.3 %collective-permute-start.3 = (f32[520,128]{1,0:T(8,128)S(1)}, f32[520,128]{1,0:T(8,128)S(1)}, u32[]{:S(2)}, u32[]{:S(2)}) collective-permute-start(f32[520,128]{1,0:T(8,128)S(1)} %get-tuple-element.28), channel_id=1, source_target_pairs={{0,1},{1,0},{2,3},{3,2},{8,16},{9,17},{10,18},{11,19},{16,8},{17,9... | collective-permute-start | bytes 798728 | tf_op jit(solution)/shard_map/ppermute | solution.py:55
  8.9 1.6 %collective-permute-start = (f32[72,128]{1,0:T(8,128)S(1)}, f32[72,128]{1,0:T(8,128)S(1)}, u32[]{:S(2)}, u32[]{:S(2)}) collective-permute-start(f32[72,128]{1,0:T(8,128)S(1)} %get-tuple-element.23), channel_id=1, source_target_pairs={{0,1},{1,0},{2,3},{3,2},{4,5},{5,4},{6,7},{7,6},{8,9},{9,8},{10,11... | collective-permute-start | bytes 110600 | tf_op jit(solution)/shard_map/ppermute | solution.py:55
  9.4 3.6 %collective-permute-start.1 = (f32[72,128]{1,0:T(8,128)S(1)}, f32[72,128]{1,0:T(8,128)S(1)}, u32[]{:S(2)}, u32[]{:S(2)}) collective-permute-start(f32[72,128]{1,0:T(8,128)S(1)} %get-tuple-element.24), channel_id=1, source_target_pairs={{0,3},{1,2},{2,1},{3,0},{4,7},{5,6},{6,5},{7,4},{8,11},{9,10},{10,... | collective-permute-start | bytes 110600 | tf_op jit(solution)/shard_map/ppermute | solution.py:55
  13.6 10.1 %copy-start.1 = (f32[3,27,8,8,128]{4,3,2,1,0:T(8,128)S(1)}, f32[3,27,8,8,128]{4,3,2,1,0:T(8,128)}, u32[]{:S(2)}) copy-start(f32[3,27,8,8,128]{4,3,2,1,0:T(8,128)} %param.4) | copy-start | bytes 7962628
  13.6 10.1 %copy-start.4 = (s32[8,8,128]{2,1,0:T(8,128)S(1)}, s32[8,8,128]{2,1,0:T(8,128)}, u32[]{:S(2)}) copy-start(s32[8,8,128]{2,1,0:T(8,128)} %param.6) | copy-start | bytes 98308
  13.6 4.5 %collective-permute-start.4 = (f32[56,128]{1,0:T(8,128)S(1)}, f32[56,128]{1,0:T(8,128)S(1)}, u32[]{:S(2)}, u32[]{:S(2)}) collective-permute-start(f32[56,128]{1,0:T(8,128)S(1)} %get-tuple-element.29), channel_id=1, source_target_pairs={{0,8},{1,9},{2,10},{3,11},{8,0},{9,1},{10,2},{11,3},{16,24},{17,25... | collective-permute-start | bytes 86024 | tf_op jit(solution)/shard_map/ppermute | solution.py:55
  16.1 2.0 %collective-permute-start.5 = (f32[56,128]{1,0:T(8,128)S(1)}, f32[56,128]{1,0:T(8,128)S(1)}, u32[]{:S(2)}, u32[]{:S(2)}) collective-permute-start(f32[56,128]{1,0:T(8,128)S(1)} %get-tuple-element.30), channel_id=1, source_target_pairs={{0,1},{1,0},{2,3},{3,2},{8,16},{9,17},{10,18},{11,19},{16,8},{17,9... | collective-permute-start | bytes 86024 | tf_op jit(solution)/shard_map/ppermute | solution.py:55
  19.3 4.4 %collective-permute-start.6 = (f32[144,128]{1,0:T(8,128)S(1)}, f32[144,128]{1,0:T(8,128)S(1)}, u32[]{:S(2)}, u32[]{:S(2)}) collective-permute-start(f32[144,128]{1,0:T(8,128)S(1)} %get-tuple-element.33), channel_id=1, source_target_pairs={{0,4},{1,5},{2,6},{3,7},{4,0},{5,1},{6,2},{7,3},{8,12},{9,13},{10,... | collective-permute-start | bytes 221192 | tf_op jit(solution)/shard_map/ppermute | solution.py:55
  26.1 4.4 %collective-permute-start.7 = (f32[144,128]{1,0:T(8,128)S(1)}, f32[144,128]{1,0:T(8,128)S(1)}, u32[]{:S(2)}, u32[]{:S(2)}) collective-permute-start(f32[144,128]{1,0:T(8,128)S(1)} %get-tuple-element.35), channel_id=1, source_target_pairs={{0,4},{1,5},{2,6},{3,7},{4,0},{5,1},{6,2},{7,3},{8,12},{9,13},{10,... | collective-permute-start | bytes 221192 | tf_op jit(solution)/shard_map/ppermute | solution.py:55
  32.5 4.4 %collective-permute-start.8 = (f32[144,128]{1,0:T(8,128)S(1)}, f32[144,128]{1,0:T(8,128)S(1)}, u32[]{:S(2)}, u32[]{:S(2)}) collective-permute-start(f32[144,128]{1,0:T(8,128)S(1)} %get-tuple-element.38), channel_id=1, source_target_pairs={{0,4},{1,5},{2,6},{3,7},{4,0},{5,1},{6,2},{7,3},{8,12},{9,13},{10,... | collective-permute-start | bytes 221192 | tf_op jit(solution)/shard_map/ppermute | solution.py:55

commit v4 on v3

v4 whole, which is shorter than its diff:
```python
import functools

import jax
import jax.numpy as jnp
import numpy as np
from jax import lax
from jax.experimental import pallas as pl
from jax.experimental.pallas import tpu as pltpu
from jax.sharding import PartitionSpec as P

STEPS = 3
DEPTH = STEPS
SLOTS = 8
Q = 27

VEL = np.array([[a, b, c] for a in (-1, 0, 1) for b in (-1, 0, 1) for c in (-1, 0, 1)])


def pop(cx, cy, cz):
    return 9 * (cx + 1) + 3 * (cy + 1) + cz + 1


U2, U1, SOLID, FLUIDITY = 27, 30, 33, 34
TRAVEL = 34


def reach(quantity, dim, toward):
    if quantity < Q:
        return DEPTH - 1 - int(VEL[quantity, dim]) * toward
    return 1 if U1 <= quantity < U1 + 3 else 2


def mirrored(quantity, dim):
    if quantity >= Q:
        return quantity
    c = [int(v) for v in VEL[quantity]]
    c[dim] = -c[dim]
    return pop(*c)


UPWARD = [(q, p) for q in range(TRAVEL) for p in range(1, reach(q, 0, 1) + 1)]


def swapped(value, axis, odd, spare):
    length = lax.axis_size(axis)
    wide = lax.axis_size(spare) if spare else 1
    pairs = []
    for i in range(length):
        for k in range(wide):
            j, m = ((i + 1 if i % 2 == 1 else i - 1) if odd else i ^ 1), k
            if not 0 <= j < length:
                j, m = (i, k ^ 1) if spare else (j % length, k)
            if j < length and m < wide:
                pairs.append((i * wide + k, j * wide + m))
    return lax.ppermute(value, (axis, spare) if spare else axis, pairs)


def both_matchings(messages, axis, spare):
    return [swapped(m, axis, k == 1, spare) for k, m in enumerate(messages)]


def matchings(axis):
    return 2 if lax.axis_size(axis) > 2 else 1


class Place:
    def __init__(self, axis):
        index = lax.axis_index(axis)
        self.even = lax.rem(index, 2) == 0
        self.lower = index > 0
        self.upper = index < lax.axis_size(axis) - 1

    def send(self, up, down):
        return jnp.where(self.even, up, down), jnp.where(self.even, down, up)

    def put(self, refs, here, up, down):
        for ref, value in zip(refs, self.send(up, down)):
            ref[here, :] = value

    def take(self, refs, here):
        first, second = refs[0][here, :], refs[-1][here, :]
        below = jnp.where(self.even, second, first)
        above = jnp.where(self.even, first, second)
        zero = jnp.zeros_like(first)
        return jnp.where(self.lower, below, zero), jnp.where(self.upper, above, zero)


class Shape:
    def __init__(self, nx, ny, nz):
        self.nx, self.ny, self.nz = nx, ny, nz
        self.rows = nz // SLOTS
        self.halo = nx + DEPTH
        if nx + 2 * DEPTH >= self.rows or nx * SLOTS * 2 > nz or nx < DEPTH or ny != 8 or self.rows % 8:
            raise ValueError("local block")

    def row(self, x):
        return x % self.rows

    def at(self, quantity, row):
        return pl.ds((quantity * self.rows + row) * self.ny, self.ny)

    def line(self, quantity, y):
        return pl.ds(quantity * self.rows * self.ny + y, self.rows, stride=self.ny)

    def raw(self, quantity, x):
        start = (quantity * self.nx + x) * self.ny
        if not isinstance(start, int):
            start = pl.multiple_of(start, self.ny)
        return pl.ds(start, self.ny)

    def raw_line(self, quantity, y):
        return pl.ds(quantity * self.nx * self.ny + y, self.nx, stride=self.ny)

    def late(self, quantity, row):
        return pl.ds((quantity * (self.rows - self.nx) + row - self.nx) * self.ny, self.ny)

    def late_line(self, quantity, y):
        count = self.rows - self.nx
        return pl.ds(quantity * count * self.ny + y, count, stride=self.ny)

    def tile(self, index):
        return pl.ds(index * self.ny, self.ny)


def lanes(g):
    return lax.broadcasted_iota(jnp.int32, (g.ny, g.nz), 1)


def roll(value, by, axis):
    size = value.shape[axis]
    if isinstance(by, int):
        by = by % size
        if by == 0:
            return value
    return pltpu.roll(value, by, axis)


def moments(load):
    total, my, mz, sums = [], [], [], {}
    for a in (-1, 0, 1):
        t, z = [], []
        for b in (-1, 0, 1):
            low, mid, high = (load(pop(a, b, c)) for c in (-1, 0, 1))
            t.append(low + mid + high)
            z.append(high - low)
        total.append(t[0] + t[1] + t[2])
        my.append(t[2] - t[0])
        mz.append(z[0] + z[1] + z[2])
    return (
        total[0] + total[1] + total[2],
        total[2] - total[0],
        my[0] + my[1] + my[2],
        mz[0] + mz[1] + mz[2],
    )


def velocity(load):
    rho, mx, my, mz = moments(load)
    inverse = 1.0 / rho
    return rho, mx * inverse, my * inverse, mz * inverse


def source(g, seed, mom, q, x):
    if q < Q:
        return seed[g.raw(q, x), :]
    return mom[g.raw({0: 1, 1: 5, 2: 8}[(q - Q) // 3] + (q - Q) % 3, x), :]


def open_kernel(g, seed_in, saved_in, porosity_in, fluid_in, seed, mom, saved, fluid, *refs):
    nx = g.nx
    *messages, porosity, sems = refs
    block = Q * nx * g.ny
    copies = [
        pltpu.make_async_copy(seed_in, seed, sems.at[0]),
        pltpu.make_async_copy(porosity_in, porosity, sems.at[1]),
        pltpu.make_async_copy(fluid_in, fluid, sems.at[2]),
        pltpu.make_async_copy(saved_in.at[pl.ds(2 * block, block), :], saved.at[pl.ds(0, block), :], sems.at[3]),
        pltpu.make_async_copy(saved_in.at[pl.ds(block, block), :], saved.at[pl.ds(block, block), :], sems.at[4]),
    ]
    for copy in copies:
        copy.start()
    lane = lanes(g)
    group, offset = lane // SLOTS, lane % SLOTS
    joint = []
    for q in range(TRAVEL):
        if q == 0:
            copies[0].wait()
        if q == Q:
            for copy in copies[1:]:
                copy.wait()

            def row(x, carry):
                here = g.raw(0, x)
                mom[g.raw(8, x), :] = jnp.where(fluid[here, :] == 1, porosity[here, :], 1.0)
                for part in range(2):
                    found = velocity(lambda i: saved[g.raw(part * Q + i, x), :])
                    for k in range(4):
                        mom[g.raw(4 * part + k, x), :] = found[k]
                return carry

            lax.fori_loop(0, nx, row, 0)
        half = (q % 2) * nx
        acc = joint.pop() if q % 2 else jnp.zeros((g.ny, g.nz), jnp.float32)
        for x in range(nx):
            moved = roll(source(g, seed, mom, q, x), (half + x) * SLOTS + DEPTH, 1)
            acc = jnp.where(group == half + x, moved, acc)
        joint.append(acc)
    z = Place("gz")
    if len(joint) % 2:
        joint.append(joint[-1])
    for k in range(len(joint) // 2):
        first, second = joint[2 * k], joint[2 * k + 1]
        up = jnp.where(offset < 4, first, roll(second, 4, 1))
        down = jnp.where(offset < 4, roll(first, -3, 1), roll(second, 1, 1))
        z.put(messages, g.tile(k), up, down)


def bulk_kernel(g, seed, mom, *messages):
    x = Place("gx")
    for k, (q, p) in enumerate(UPWARD):
        up, down = source(g, seed, mom, q, g.nx - p), source(g, seed, mom, mirrored(q, 0), p - 1)
        x.put(messages, g.tile(k), up, down)


def place_kernel(g, mom, saved_in, extra, mom0, saved, sem):
    nx = g.nx
    fetch = pltpu.make_async_copy(saved_in.at[pl.ds(0, Q * nx * g.ny), :], saved, sem)
    fetch.start()
    for x in range(nx):
        for k in range(3):
            extra[g.raw(k, x), :] = mom[g.raw(1 + k, x), :]
            extra[g.raw(3 + k, x), :] = mom[g.raw(5 + k, x), :]
        solid = mom[g.raw(8, x), :]
        extra[g.raw(6, x), :] = solid
        extra[g.raw(7, x), :] = 1.0 - solid
    fetch.wait()

    def row(x, carry):
        found = velocity(lambda i: saved[g.raw(i, x), :])
        for k in range(4):
            mom0[g.raw(k, x), :] = found[k]
        return carry

    lax.fori_loop(0, nx, row, 0)


def swap_edges(g, i, row, own, edge):
    lane = lanes(g)
    cz = int(VEL[i, 2])
    if cz == 0:
        return own, edge
    slot = row * SLOTS
    if cz > 0:
        here, out, back = 0, slot + DEPTH + 2, slot + DEPTH
    else:
        here, out, back = g.nz - 1, slot + DEPTH - 1, slot + DEPTH + 1
    return (
        jnp.where(lane == here, roll(edge, here - out, 1), own),
        jnp.where(lane == back, roll(own, back - here, 1), edge),
    )


def second_kernel(g, *refs):
    nx = g.nx
    heard, halo, messages = refs[: matchings("gz")], refs[matchings("gz")], refs[matchings("gz") + 1 :]
    lane = lanes(g)
    group, offset = lane // SLOTS, lane % SLOTS
    z, x = Place("gz"), Place("gx")
    below, above = [], []
    for k in range(-(-TRAVEL // 4)):
        low, high = z.take(heard, g.tile(k))
        below.append(low)
        above.append(high)
    tiles = []
    for q in range(TRAVEL):
        at = (q % 2) * nx * SLOTS + (q // 2 % 2) * 4
        low = roll(below[q // 4], -at, 1)
        high = roll(above[q // 4], DEPTH + 2 - at, 1)
        tiles.append(jnp.where(group < nx, jnp.where(offset < 4, low, high), 0.0))
        halo[g.tile(q), :] = tiles[-1]
    width = DEPTH * SLOTS
    per = g.nz // width
    for k in range(-(-TRAVEL // per)):
        up = down = jnp.zeros((g.ny, g.nz), jnp.float32)
        for j in range(min(per, TRAVEL - k * per)):
            tile = tiles[k * per + j]
            part = (lane >= j * width) & (lane < (j + 1) * width)
            up = jnp.where(part, roll(tile, j * width - (nx - DEPTH) * SLOTS, 1), up)
            down = jnp.where(part, roll(tile, j * width, 1), down)
        x.put(messages, g.tile(k), up, down)


def edges_kernel(g, seed, halo, field, turned, up, down):
    for i in range(Q):
        edge = halo[g.tile(i), :]
        for x in range(g.nx):
            own, edge = swap_edges(g, i, x, seed[g.raw(i, x), :], edge)
            field[g.raw(i, x), :] = own
        turned[g.tile(i), :] = edge
    for k in range(9):
        a, c = k // 3 - 1, k % 3 - 1
        here = pl.ds(k * g.nx, g.nx)
        up[here, :] = field[g.raw_line(pop(a, -1, c), g.ny - 1), :]
        down[here, :] = field[g.raw_line(pop(a, 1, c), 0), :]


def rows_kernel(g, *refs):
    *heard, field, extra = refs
    x = Place("gx")
    for k, (q, p) in enumerate(UPWARD):
        low, high = x.take(heard, g.tile(k))
        for index, row, value, there in (
            (q, g.row(-p), low, x.lower),
            (mirrored(q, 0), g.row(g.nx - 1 + p), high, x.upper),
        ):
            if index < Q:
                field[g.late(index, row), :] = value
            else:
                extra[g.late(index - Q, row), :] = value
            if index == SOLID:
                extra[g.late(7, row), :] = jnp.where(there, 1.0 - value, 0.0)


def third_kernel(g, turned, halo, rows, extras, up, down, *refs):
    nx = g.nx
    heard, (field, extra, *messages) = refs[: matchings("gx")], refs[matchings("gx") :]
    x, y, z = Place("gx"), Place("gy"), Place("gz")
    lane = lanes(g)
    group, offset = lane // SLOTS, lane % SLOTS

    def target(q):
        return (field, q) if q < Q else (extra, q - Q)

    lower, upper = group >= g.rows - DEPTH, (group >= nx) & (group < nx + DEPTH)
    width = DEPTH * SLOTS
    per = g.nz // width
    edges = []
    for k in range(-(-TRAVEL // per)):
        low, high = x.take(heard, g.tile(k))
        for j in range(min(per, TRAVEL - k * per)):
            q = k * per + j
            tile = turned[g.tile(q), :] if q < Q else halo[g.tile(q), :]
            tile = jnp.where(lower, roll(low, (g.rows - DEPTH) * SLOTS - j * width, 1), tile)
            edges.append(jnp.where(upper, roll(high, nx * SLOTS - j * width, 1), tile))
    extra[...] = extras[...]
    for q in range(TRAVEL):
        ref, index = target(q)
        edge = edges[q]
        if q < Q:
            for p in range(1, DEPTH + 1):
                for row, toward in ((g.row(-p), 1), (nx - 1 + p, -1)):
                    if p > reach(q, 0, toward):
                        continue
                    own, edge = swap_edges(g, q, row, rows[g.late(q, row), :], edge)
                    field[g.late(q, row), :] = own
        ref[g.late(index, g.halo), :] = edge
    there = jnp.where(lower, jnp.where(x.lower, 1, 0), jnp.where(upper, jnp.where(x.upper, 1, 0), 1))
    there = there * jnp.where(offset < 4, jnp.where(z.lower, 1, 0), jnp.where(z.upper, 1, 0))
    extra[g.late(7, g.halo), :] = jnp.where(there == 1, 1.0 - edges[SOLID], 0.0)
    for k in range(9):
        a, c = k // 3 - 1, k % 3 - 1
        for late in (False, True):
            here = pl.ds(k * g.rows + late * nx, g.rows - nx if late else nx)
            if late:
                sent = field[g.late_line(pop(a, -1, c), g.ny - 1), :], field[g.late_line(pop(a, 1, c), 0), :]
            else:
                sent = up[pl.ds(k * nx, nx), :], down[pl.ds(k * nx, nx), :]
            y.put(messages, here, *sent)


def pulled_moments(p):
    t = {}
    for a in (-1, 0, 1):
        s0, s1, s2 = [], [], []
        for b in (-1, 0, 1):
            low, mid, high = (p[pop(a, b, c)] for c in (-1, 0, 1))
            both = low + high
            s0.append(4.0 * mid + both)
            s1.append(high - low)
            s2.append(both)
        both = s0[0] + s0[2]
        t[a] = (
            4.0 * s0[1] + both,
            s0[2] - s0[0],
            both,
            4.0 * s1[1] + (s1[0] + s1[2]),
            s1[2] - s1[0],
            4.0 * s2[1] + (s2[0] + s2[2]),
        )
    both = [t[-1][k] + t[1][k] for k in range(6)]
    full = [4.0 * t[0][k] + both[k] for k in range(6)]
    m0, my, myy, mz, myz, mzz = full
    mx, mxx = t[1][0] - t[-1][0], both[0]
    mxy, mxz = t[1][1] - t[-1][1], t[1][3] - t[-1][3]
    return m0, mx, my, mz, mxx, myy, mzz, mxy, mxz, myz


def edge_moments(p, side):
    t = {}
    for a in (-1, 0, 1):
        low, mid, high = (p[pop(a, side, c)] for c in (-1, 0, 1))
        both = low + high
        t[a] = (4.0 * mid + both, high - low, both)
    both = [t[-1][k] + t[1][k] for k in range(3)]
    m0, mz, mzz = (4.0 * t[0][k] + both[k] for k in range(3))
    mx, mxz = t[1][0] - t[-1][0], t[1][1] - t[-1][1]
    if side > 0:
        return m0, mx, m0, mz, both[0], m0, mzz, mx, mxz, mz
    return m0, mx, -m0, mz, both[0], m0, mzz, -mx, mxz, -mz


def transposed(p, u, solid, fluidity, side=0):
    found = edge_moments(p, side) if side else pulled_moments(p)
    m0, mx, my, mz, mxx, myy, mzz, mxy, mxz, myz = found
    ux, uy, uz = u
    usq = ux * ux + uy * uy + uz * uz
    vx = mxx * ux + mxy * uy + mxz * uz
    vy = mxy * ux + myy * uy + myz * uz
    vz = mxz * ux + myz * uy + mzz * uz
    quad = ux * vx + uy * vy + uz * vz
    scale = fluidity * (1.6 / 216.0)
    kept = -0.6 * fluidity
    base = scale * (m0 + 1.5 * usq * m0 - 4.5 * quad)
    bx = scale * (3.0 * (mx - ux * m0) + 9.0 * vx)
    by = scale * (3.0 * (my - uy * m0) + 9.0 * vy)
    bz = scale * (3.0 * (mz - uz * m0) + 9.0 * vz)
    out = [None] * Q
    for a in (-1, 0, 1):
        ga = base + bx if a > 0 else (base - bx if a < 0 else base)
        for b in (-1, 0, 1):
            gb = ga + by if b > 0 else (ga - by if b < 0 else ga)
            for c in (-1, 0, 1):
                gc = gb + bz if c > 0 else (gb - bz if c < 0 else gb)
                i = pop(a, b, c)
                if not side or b == side:
                    gc = kept * p[i] + gc
                if not side or b == -side:
                    gc = solid * p[Q - 1 - i] + gc
                out[i] = gc
    flow = m0 * (1.0 - 1.5 * usq) + 3.0 * (ux * mx + uy * my + uz * mz) + 4.5 * quad
    return out, flow


def inner_kernel(g, step, early, late, extra, extra_late, mom, saved, fluid, grad, *refs):
    nx = g.nx
    base, part_at = 3 * (2 - step), (Q if step == 1 else 0)
    lines = refs[:2] if step < STEPS - 1 else None
    *outs, field = refs[2:] if lines else refs
    zero = jnp.zeros((g.rows, g.nz), jnp.float32)
    for i in range(Q):
        for row in range(g.rows):
            field[g.at(i, row), :] = early[g.raw(i, row), :] if row < nx else late[g.late(i, row), :]
        if VEL[i, 1] < 0:
            field[g.line(i, g.ny - 1), :] = zero
        elif lines:
            field[g.line(i, g.ny - 1), :] = lines[0][pl.ds(i * g.rows, g.rows), :]
        if VEL[i, 1] > 0:
            field[g.line(i, 0), :] = zero
        elif lines:
            field[g.line(i, 0), :] = lines[1][pl.ds(i * g.rows, g.rows), :]

    def part(k, row):
        return extra[g.raw(k, row), :] if row < nx else extra_late[g.late(k, row), :]

    def parts(row):
        return [part(k, row) for k in (base, base + 1, base + 2, 6, 7)]

    def pull(row):
        return [
            roll(
                roll(field[g.at(i, g.row(row + int(VEL[i, 0]))), :], -int(VEL[i, 2]), 1),
                -int(VEL[i, 1]),
                0,
            )
            for i in range(Q)
        ]

    if step:
        next_early, next_late, grad_out = outs
        p = [
            roll(
                roll(field[g.at(i, g.halo), :], -(SLOTS * int(VEL[i, 0]) + int(VEL[i, 2])), 1),
                -int(VEL[i, 1]),
                0,
            )
            for i in range(Q)
        ]
        *u, solid, fluidity = parts(g.halo)
        out, _ = transposed(p, u, solid, fluidity)
        for i in range(Q):
            next_late[g.late(i, g.halo), :] = out[i]
    else:
        result, up, down, grad_out = outs

    for x in range(-step, nx + step):
        row, local = g.row(x), 0 <= x < nx
        p = pull(row)
        if step:
            *u, solid, fluidity = parts(row)
        else:
            u = [mom[g.raw(1 + k, x), :] for k in range(3)]
            solid, fluidity = part(6, row), part(7, row)
        out, flow = transposed(p, u, solid, fluidity)
        if local:
            rho = mom[g.raw(4 * (2 - step) if step else 0, x), :]
            same = cross = None
            for i in range(Q):
                f = saved[g.raw(part_at + i, x), :]
                one, two = p[i] * f, p[Q - 1 - i] * f
                same, cross = (one, two) if same is None else (same + one, cross + two)
            term = 0.6 * same + cross - (1.6 / 216.0) * (rho * flow)
            here = g.tile(x)
            grad_out[here, :] = jnp.where(fluid[here, :] == 1, grad[here, :] + term, 0.0)
        for i in range(Q):
            if step:
                here = g.late(i, g.halo)
                own, edge = swap_edges(g, i, row, out[i], next_late[here, :])
                if VEL[i, 2]:
                    next_late[here, :] = edge
                if row < nx:
                    next_early[g.raw(i, row), :] = own
                else:
                    next_late[g.late(i, row), :] = own
            else:
                result[g.raw(i, x), :] = out[i]
    if not step:
        for i in range(Q):
            here = pl.ds(i * nx, nx)
            up[here, :] = result[g.raw_line(i, g.ny - 1), :]
            down[here, :] = result[g.raw_line(i, 0), :]


def edge_kernel(g, step, sending, *refs):
    nx = g.nx
    y = Place("gy")
    base = 3 * (2 - step)
    sub = lax.broadcasted_iota(jnp.int32, (g.rows, g.nz), 0)
    lane = lax.broadcasted_iota(jnp.int32, (g.rows, g.nz), 1)
    part_at = Q if step == 1 else 0
    heard, refs = refs[: matchings("gy")], refs[matchings("gy") :]
    early, late, extra, extra_late, mom, *refs = refs
    if sending:
        *messages, up, down = refs
    elif step:
        saved, fluid, grad_in, up, down, grad = refs
    else:
        saved, fluid, grad_in, _, whole, grad, up, down, sems = refs
    if not sending:
        grad[...] = grad_in[...]

    def wanted(side):
        return [i for i in range(Q) if not sending or VEL[i, 1] == -side]

    def joined(first, second, k, edge):
        return jnp.concatenate([first[g.raw_line(k, edge), :], second[g.late_line(k, edge), :]], axis=0)

    def swapped_edges(i, tile):
        cz = int(VEL[i, 2])
        here, out, back = (0, DEPTH + 2, DEPTH) if cz > 0 else (g.nz - 1, DEPTH - 1, DEPTH + 1)
        own = jnp.broadcast_to(tile[:, here : here + 1], tile.shape)
        edge = jnp.broadcast_to(tile[g.halo : g.halo + 1, :], tile.shape)
        column = jnp.sum(jnp.where(lane == sub * SLOTS + out, edge, 0.0), axis=1, keepdims=True)
        line = jnp.sum(jnp.where(lane == sub * SLOTS + back, own, 0.0), axis=0, keepdims=True)
        tile = jnp.where((lane == here) & (sub != g.halo), column, tile)
        return jnp.where((sub == g.halo) & (lane % SLOTS == back), line, tile)

    def before(i, side):
        if step:
            return joined(early, late, i, g.ny - 1 if side > 0 else 0)
        return (early if side > 0 else late)[pl.ds(i * nx, nx), :]

    def store(side, i, value):
        count = g.rows if step else nx
        (up if side > 0 else down)[pl.ds(i * count, count), :] = value

    def correct(side):
        edge = g.ny - 1 if side > 0 else 0
        p = [None] * Q
        for k in range(9):
            a, c = k // 3 - 1, k % 3 - 1
            here = pl.ds(k * g.rows, g.rows)
            first, second = heard[0][here, :], heard[-1][here, :]
            value = jnp.where(y.even if side > 0 else jnp.logical_not(y.even), first, second)
            moved = roll(roll(value, -a, 0), -c, 1)
            if step:
                moved = jnp.where(sub == g.halo, roll(value, -(SLOTS * a + c), 1), moved)
            else:
                moved = moved[:nx]
            p[pop(a, side, c)] = moved
        if step:
            *u, solid, fluidity = (joined(extra, extra_late, k, edge) for k in (base, base + 1, base + 2, 6, 7))
        else:
            u = [mom[g.raw_line(1 + k, edge), :] for k in range(3)]
            solid, fluidity = (extra[g.raw_line(k, edge), :] for k in (6, 7))
        out, flow = transposed(p, u, solid, fluidity, side)
        for i in wanted(side):
            tile = swapped_edges(i, out[i]) if step and VEL[i, 2] else out[i]
            store(side, i, before(i, side) + tile)
        if sending:
            return
        rho = mom[g.raw_line(4 * (2 - step) if step else 0, edge), :]
        same = cross = None
        for i in range(Q):
            if VEL[i, 1] != side:
                continue
            value = p[i][:nx]
            one = value * saved[g.raw_line(part_at + i, edge), :]
            two = value * saved[g.raw_line(part_at + Q - 1 - i, edge), :]
            same, cross = (one, two) if same is None else (same + one, cross + two)
        term = 0.6 * same + cross - (1.6 / 216.0) * (rho * flow[:nx])
        at = g.raw_line(0, edge)
        grad[at, :] = jnp.where(fluid[at, :] == 1, grad_in[at, :] + term, 0.0)

    def write(side):
        edge = g.ny - 1 if side > 0 else 0
        return pltpu.make_async_copy(up if side > 0 else down, whole.at[:, edge, :], sems.at[0 if side > 0 else 1])

    for side, there in ((1, y.upper), (-1, y.lower)):

        @pl.when(there)
        def _(side=side):
            correct(side)
            if not step:
                write(side).start()

        if step:

            @pl.when(jnp.logical_not(there))
            def _(side=side):
                for i in wanted(side):
                    store(side, i, before(i, side))

    if sending:
        for k in range(9):
            a, c = k // 3 - 1, k % 3 - 1
            here = pl.ds(k * g.rows, g.rows)
            sent = (up, pop(a, -1, c)), (down, pop(a, 1, c))
            y.put(messages, here, *(ref[pl.ds(i * g.rows, g.rows), :] for ref, i in sent))
    elif not step:
        for side, there in ((1, y.upper), (-1, y.lower)):

            @pl.when(there)
            def _(side=side):
                write(side).wait()


def call(kernel, name, outs, args, flops, aliases=None, scratch=(), spaces=None, out_spaces=None):
    moved = 4 * sum(int(np.prod(a.shape)) for a in [*args, *outs])
    spaces = spaces or [pltpu.VMEM] * len(args)
    out_spaces = out_spaces or [pltpu.VMEM] * len(outs)
    return pl.pallas_call(
        kernel,
        name=name,
        out_shape=outs,
        in_specs=[pl.BlockSpec(memory_space=m) for m in spaces],
        out_specs=[pl.BlockSpec(memory_space=m) for m in out_spaces],
        scratch_shapes=scratch,
        input_output_aliases=aliases or {},
        compiler_params=pltpu.CompilerParams(vmem_limit_bytes=VMEM_LIMIT),
        cost_estimate=pl.CostEstimate(flops=flops, bytes_accessed=moved, transcendentals=0),
    )(*args)


VMEM_LIMIT = 24 * 1024 * 1024


def local(saved, porosity, fluid, seed_adjoint):
    nx, ny, nz = porosity.shape
    g = Shape(nx, ny, nz)
    bind = functools.partial
    f32 = lambda *shape: jax.ShapeDtypeStruct(shape, jnp.float32)
    seed = seed_adjoint.reshape(Q * nx * ny, nz)
    pops = saved.reshape(STEPS * Q * nx * ny, nz)
    porosity = porosity.reshape(nx * ny, nz)
    fluid = fluid.reshape(nx * ny, nz)
    voxels, rest = nx * ny * nz, (g.rows - nx) * ny
    flat, full, late = f32(nx * ny, nz), f32(Q * nx * ny, nz), f32(Q * rest, nz)
    zs = f32(-(-TRAVEL // 4) * ny, nz)
    xs = f32(len(UPWARD) * ny, nz)
    ss = f32(-(-TRAVEL // (nz // (DEPTH * SLOTS))) * ny, nz)
    ys, yl, lines = f32(9 * g.rows, nz), f32(9 * nx, nz), f32(Q * g.rows, nz)

    hbm = lambda *values: [pltpu.with_memory_space_constraint(v, pltpu.HBM) for v in values]
    nmx, nmy, nmz = (matchings(axis) for axis in ("gx", "gy", "gz"))
    seed, mom, late_pops, fluid, *zm = call(
        bind(open_kernel, g), "open",
        [full, f32(9 * nx * ny, nz), f32(2 * Q * nx * ny, nz), jax.ShapeDtypeStruct((nx * ny, nz), jnp.int32), *[zs] * nmz],
        hbm(seed, pops, porosity, fluid), 200 * voxels, spaces=[pltpu.HBM] * 4,
        scratch=[pltpu.VMEM((nx * ny, nz), jnp.float32), pltpu.SemaphoreType.DMA((5,))],
    )
    with jax.named_scope("zswap"):
        zm = both_matchings(zm, "gz", None)
    with jax.named_scope("bulk"):
        xm = call(bind(bulk_kernel, g), "bulk", [xs] * nmx, [seed, mom], 10 * voxels)
    with jax.named_scope("xswap"):
        xm = both_matchings(xm, "gx", "gz")
    extra, mom0, first_pops = call(
        bind(place_kernel, g), "place", [f32(8 * nx * ny, nz), f32(4 * nx * ny, nz), full],
        [mom, *hbm(pops)], 50 * voxels, spaces=[pltpu.VMEM, pltpu.HBM], scratch=[pltpu.SemaphoreType.DMA(())],
    )
    halo, *sm = call(bind(second_kernel, g), "second", [f32(TRAVEL * ny, nz), *[ss] * nmx], zm, 20 * voxels)
    with jax.named_scope("smallswap"):
        sm = both_matchings(sm, "gx", "gz")
    early, turned, up, down = call(
        bind(edges_kernel, g), "edges", [full, f32(Q * ny, nz), yl, yl], [seed, halo], 50 * voxels
    )
    rows, extra_rows = call(bind(rows_kernel, g), "rows", [late, f32(8 * rest, nz)], xm, 20 * voxels)
    late_rows, extra_late, *ym = call(
        bind(third_kernel, g), "third", [late, f32(8 * rest, nz), *[ys] * nmy],
        [turned, halo, rows, extra_rows, up, down, *sm], 50 * voxels,
    )
    grad = jnp.zeros((nx * ny, nz), jnp.float32)
    field, lined = [early, late_rows], []
    for step in (2, 1, 0):
        ym = both_matchings(ym, "gy", "gz")
        state = [extra, extra_late, mom if step else mom0]
        kept = [late_pops if step else first_pops, fluid]
        scratch = [pltpu.VMEM((Q * g.rows * ny, nz), jnp.float32)]
        args = [*field, *state, *kept, grad, *lined]
        if step:
            *field, grad = call(
                bind(inner_kernel, g, step), f"inner{step}", [full, late, flat], args, 400 * voxels, scratch=scratch
            )
            args = [*ym, *field, *state]
            ym = call(
                bind(edge_kernel, g, step, True), f"send{step}", [ys] * nmy, args, 20 * voxels,
                scratch=[pltpu.VMEM((Q * g.rows, nz), jnp.float32)] * 2,
            )
            up, down, grad = call(
                bind(edge_kernel, g, step, False), f"edge{step}", [lines, lines, flat], [*args, *kept, grad], 40 * voxels
            )
            lined = [up, down]
            continue
        part = f32(Q * nx, nz)
        whole, up, down, grad = call(
            bind(inner_kernel, g, step), f"inner{step}", [full, part, part, flat], args, 400 * voxels, scratch=scratch
        )
        args = [*ym, up, down, *state, *kept, grad, whole.reshape(Q * nx, ny, nz)]
        adjoint, grad = call(
            bind(edge_kernel, g, step, False), f"edge{step}", [f32(Q * nx, ny, nz), flat], args, 40 * voxels,
            {len(args) - 1: 0}, spaces=[*[pltpu.VMEM] * (len(args) - 1), pltpu.HBM], out_spaces=[pltpu.HBM, pltpu.VMEM],
            scratch=[pltpu.VMEM((Q * nx, nz), jnp.float32)] * 2 + [pltpu.SemaphoreType.DMA((2,))],
        )
    return adjoint.reshape(Q, nx, ny, nz), grad.reshape(nx, ny, nz)


def solution(mesh):
    return jax.shard_map(
        local,
        mesh=mesh,
        in_specs=(
            P(None, None, "gx", "gy", "gz"),
            P("gx", "gy", "gz"),
            P("gx", "gy", "gz"),
            P(None, "gx", "gy", "gz"),
        ),
        out_specs=(P(None, "gx", "gy", "gz"), P("gx", "gy", "gz")),
        check_vma=False,
    )
```

time: 39.2 us -> 31.3 us (0.80)
  waiting for transfers between devices: 12.5 us -> 5.94 us
  local copies, waits for them, and re-layouts: 4.44 us -> 0.01 us
  Pallas kernels: 8.99 us -> 12.8 us
  starting transfers between devices: 12.3 us -> 11.6 us
    ppermute x9, waiting for transfers between devices: 12.5 us -> 5.94 us  [swapped(): return lax.ppermute(value, (axis, spare) if spare else axis, pairs)]
    unnamed x12 -> x0, local copies, waits for them, and re-layouts: 4.44 us -> none
    pallas_call x6 -> x15, Pallas kernels: 8.99 us -> 12.8 us  [call(): pl.pallas_call(kernel, name=name, out_shape=outs, in_specs=[pl.BlockSpec(...]
    ppermute x9, starting transfers between devices: 12.3 us -> 11.6 us  [swapped(): return lax.ppermute(value, (axis, spare) if spare else axis, pairs)]
  transfers between devices with their start and end apart: 9 -> 9, of which waited for: 5 -> 4; matrix products, arithmetic and copies ran while one was open for 0% -> 0% of each run, Pallas kernels for 1% -> 26%
where the time goes in v4:
time: 31.3 us; the launch traced here: 31.1 us
  Pallas kernels  12.8 us (41%)
  starting transfers between devices  11.6 us (37%)
  waiting for transfers between devices  5.94 us (19%)
  between operations  0.76 us (2%)
    pallas_call x15, Pallas kernels, call(): pl.pallas_call(kernel, name=name, out_shape=outs, in_specs=[pl.BlockSpec(...  12.8 us
    ppermute x9, starting transfers between devices, swapped(): return lax.ppermute(value, (axis, spare) if spare else axis, pairs)  11.6 us
    ppermute x9, waiting for transfers between devices, swapped(): return lax.ppermute(value, (axis, spare) if spare else axis, pairs)  5.94 us
  transfers between devices with their start and end apart: 9, of which 4 were waited for; matrix products, arithmetic and copies ran while one was open for 0% of the time, Pallas kernels for 26%

profile of v4, /device:TPU:0, one launch (start us, length us, event | category | flops | bytes accessed | tf_op | source)
XLA Modules:
  0.0 31.1 jit_solution(8985448609580684057)
XLA Ops:
  0.6 2.3 %open.1 = (f32[1728,128]{1,0:T(8,128)S(1)}, f32[576,128]{1,0:T(8,128)S(1)}, f32[3456,128]{1,0:T(8,128)S(1)}, s32[64,128]{1,0:T(8,128)S(1)}, f32[72,128]{1,0:T(8,128)S(1)}, /*index=5*/f32[72,128]{1,0:T(8,128)S(1)}) custom-call(f32[1728,128]{1,0:T(8,128)} %bitcast.9, f32[5184,128]{1,0:T(8,128)} %bitcast.7, f32[64,128]{1,0:T(8,128)} %bitcast.12, s32[64,128]{1,0:T(8,128)} %bitcast.13), custom_call_target="tpu_custom_call" | custom-call | flops 1638400 | bytes 6660096 | tf_op jit(solution)/shard_map/open/pallas_call | solution.py:651
  2.9 0.1 bulk.1
  3.0 3.1 %collective-permute-start.2 = (f32[520,128]{1,0:T(8,128)S(1)}, f32[520,128]{1,0:T(8,128)S(1)}, u32[]{:S(2)}, u32[]{:S(2)}) collective-permute-start(f32[520,128]{1,0:T(8,128)S(1)} %get-tuple-element.49), channel_id=1, source_target_pairs={{0,8},{1,9},{2,10},{3,11},{8,0},{9,1},{10,2},{11,3},{16,24},{17,25... | collective-permute-start | bytes 798728 | tf_op jit(solution)/shard_map/xswap/ppermute | solution.py:55
  6.1 0.0 collective-permute-start.3
  6.1 0.5 %collective-permute-start = (f32[72,128]{1,0:T(8,128)S(1)}, f32[72,128]{1,0:T(8,128)S(1)}, u32[]{:S(2)}, u32[]{:S(2)}) collective-permute-start(f32[72,128]{1,0:T(8,128)S(1)} %get-tuple-element.44), channel_id=1, source_target_pairs={{0,1},{1,0},{2,3},{3,2},{4,5},{5,4},{6,7},{7,6},{8,9},{9,8},{10,11... | collective-permute-start | bytes 110600 | tf_op jit(solution)/shard_map/zswap/ppermute | solution.py:55
  6.6 1.1 %collective-permute-start.1 = (f32[72,128]{1,0:T(8,128)S(1)}, f32[72,128]{1,0:T(8,128)S(1)}, u32[]{:S(2)}, u32[]{:S(2)}) collective-permute-start(f32[72,128]{1,0:T(8,128)S(1)} %get-tuple-element.45), channel_id=1, source_target_pairs={{0,3},{1,2},{2,1},{3,0},{4,7},{5,6},{6,5},{7,4},{8,11},{9,10},{10,... | collective-permute-start | bytes 110600 | tf_op jit(solution)/shard_map/zswap/ppermute | solution.py:55
  7.7 0.0 collective-permute-done.refs_0_
  7.7 2.5 %collective-permute-done.1.refs_1_ = f32[72,128]{1,0:T(8,128)S(1)} collective-permute-done((f32[72,128]{1,0:T(8,128)S(1)}, f32[72,128]{1,0:T(8,128)S(1)}, u32[]{:S(2)}, u32[]{:S(2)}) %collective-permute-start.1) | collective-permute-done | bytes 36896 | tf_op jit(solution)/shard_map/zswap/ppermute | solution.py:55
  10.2 0.2 second.1
  10.5 2.5 %collective-permute-start.4 = (f32[56,128]{1,0:T(8,128)S(1)}, f32[56,128]{1,0:T(8,128)S(1)}, u32[]{:S(2)}, u32[]{:S(2)}) collective-permute-start(f32[56,128]{1,0:T(8,128)S(1)} %get-tuple-element.55), channel_id=1, source_target_pairs={{0,8},{1,9},{2,10},{3,11},{8,0},{9,1},{10,2},{11,3},{16,24},{17,25... | collective-permute-start | bytes 86024 | tf_op jit(solution)/shard_map/smallswap/ppermute | solution.py:55
  13.0 0.5 %collective-permute-start.5 = (f32[56,128]{1,0:T(8,128)S(1)}, f32[56,128]{1,0:T(8,128)S(1)}, u32[]{:S(2)}, u32[]{:S(2)}) collective-permute-start(f32[56,128]{1,0:T(8,128)S(1)} %get-tuple-element.56), channel_id=1, source_target_pairs={{0,1},{1,0},{2,3},{3,2},{8,16},{9,17},{10,18},{11,19},{16,8},{17,9... | collective-permute-start | bytes 86024 | tf_op jit(solution)/shard_map/smallswap/ppermute | solution.py:55
  13.5 0.6 %edges.1 = (f32[1728,128]{1,0:T(8,128)S(1)}, f32[216,128]{1,0:T(8,128)S(1)}, f32[72,128]{1,0:T(8,128)S(1)}, f32[72,128]{1,0:T(8,128)S(1)}) custom-call(f32[1728,128]{1,0:T(8,128)S(1)} %get-tuple-element.43.seed, f32[272,128]{1,0:T(8,128)S(1)} %get-tuple-element.46.halo), custom_call_target="tpu_custom_call" | custom-call | flops 409600 | bytes 2093056 | tf_op jit(solution)/shard_map/edges/pallas_call | solution.py:651
  14.1 0.0 collective-permute-done.3.refs_1_
  14.1 0.1 rows.1
  14.1 0.9 %collective-permute-done.4.refs_0_ = f32[56,128]{1,0:T(8,128)S(1)} collective-permute-done((f32[56,128]{1,0:T(8,128)S(1)}, f32[56,128]{1,0:T(8,128)S(1)}, u32[]{:S(2)}, u32[]{:S(2)}) %collective-permute-start.4) | collective-permute-done | bytes 28704 | tf_op jit(solution)/shard_map/smallswap/ppermute | solution.py:55
  15.0 0.0 collective-permute-done.5.refs_1_
  15.0 0.5 %third.1 = (f32[1728,128]{1,0:T(8,128)S(1)}, f32[512,128]{1,0:T(8,128)S(1)}, f32[144,128]{1,0:T(8,128)S(1)}) custom-call(f32[216,128]{1,0:T(8,128)S(1)} %get-tuple-element.47.turned, f32[272,128]{1,0:T(8,128)S(1)} %get-tuple-element.46.halo, f32[1728,128]{1,0:T(8,128)S(1)} %get-tuple-element.51.rows, f32[512,128]{1,0:T(8,128)S(1)} %get-tuple-element.52.extras, ...), custom_call_target="tpu_custom_call" | custom-call | flops 409600 | bytes 2748416 | tf_op jit(solution)/shard_map/third/pallas_call | solution.py:651
  15.5 1.6 %collective-permute-start.6 = (f32[144,128]{1,0:T(8,128)S(1)}, f32[144,128]{1,0:T(8,128)S(1)}, u32[]{:S(2)}, u32[]{:S(2)}) collective-permute-start(f32[144,128]{1,0:T(8,128)S(1)} %get-tuple-element.57), channel_id=1, source_target_pairs={{0,4},{1,5},{2,6},{3,7},{4,0},{5,1},{6,2},{7,3},{8,12},{9,13},{10,... | collective-permute-start | bytes 221192 | tf_op jit(solution)/shard_map/ppermute | solution.py:55
  17.1 1.4 %place.1 = (f32[512,128]{1,0:T(8,128)S(1)}, f32[256,128]{1,0:T(8,128)S(1)}, f32[1728,128]{1,0:T(8,128)S(1)}) custom-call(f32[576,128]{1,0:T(8,128)S(1)} %get-tuple-element.48.mom.refs_5_, f32[5184,128]{1,0:T(8,128)} %bitcast.8), custom_call_target="tpu_custom_call" | custom-call | flops 409600 | bytes 4227072 | tf_op jit(solution)/shard_map/place/pallas_call | solution.py:651
  18.5 1.8 %inner2.1 = (f32[1728,128]{1,0:T(8,128)S(1)}, f32[1728,128]{1,0:T(8,128)S(1)}, f32[64,128]{1,0:T(8,128)S(1)}) custom-call(f32[1728,128]{1,0:T(8,128)S(1)} %get-tuple-element.58.early, f32[1728,128]{1,0:T(8,128)S(1)} %get-tuple-element.59.late, f32[512,128]{1,0:T(8,128)S(1)} %get-tuple-element.60.extra.refs_3_, ...), custom_call_target="tpu_custom_call" | custom-call | flops 3276800 | bytes 6225920 | tf_op jit(solution)/shard_map/inner2/pallas_call | solution.py:651
  20.3 0.0 collective-permute-done.6.refs_0_
  20.3 0.3 send2.1
  20.6 1.1 %collective-permute-start.7 = (f32[144,128]{1,0:T(8,128)S(1)}, f32[144,128]{1,0:T(8,128)S(1)}, u32[]{:S(2)}, u32[]{:S(2)}) collective-permute-start(f32[144,128]{1,0:T(8,128)S(1)} %send2.1), channel_id=1, source_target_pairs={{0,4},{1,5},{2,6},{3,7},{4,0},{5,1},{6,2},{7,3},{8,12},{9,13},{10,... | collective-permute-start | bytes 221192 | tf_op jit(solution)/shard_map/ppermute | solution.py:55
  21.8 0.4 %edge2.1 = (f32[432,128]{1,0:T(8,128)S(1)}, f32[432,128]{1,0:T(8,128)S(1)}, f32[64,128]{1,0:T(8,128)S(1)}) custom-call(f32[144,128]{1,0:T(8,128)S(1)} %collective-permute-done.6.refs_0_, f32[1728,128]{1,0:T(8,128)S(1)} %get-tuple-element.64.refs_1_.early, f32[1728,128]{1,0:T(8,128)S(1)} %get-tuple-element.65.refs_2_.late, ...), custom_call_target="tpu_custom_call" | custom-call | flops 327680 | bytes 4972544 | tf_op jit(solution)/shard_map/edge2/pallas_call | solution.py:651
  22.2 1.6 %inner1.1 = (f32[1728,128]{1,0:T(8,128)S(1)}, f32[1728,128]{1,0:T(8,128)S(1)}, f32[64,128]{1,0:T(8,128)S(1)}) custom-call(f32[1728,128]{1,0:T(8,128)S(1)} %get-tuple-element.64.refs_1_.early, f32[1728,128]{1,0:T(8,128)S(1)} %get-tuple-element.65.refs_2_.late, f32[512,128]{1,0:T(8,128)S(1)} %get-tuple-element.60.extra.refs_3_, ...), custom_call_target="tpu_custom_call" | custom-call | flops 3276800 | bytes 6668288 | tf_op jit(solution)/shard_map/inner1/pallas_call | solution.py:651
  23.7 1.3 %collective-permute-done.7.refs_0_ = f32[144,128]{1,0:T(8,128)S(1)} collective-permute-done((f32[144,128]{1,0:T(8,128)S(1)}, f32[144,128]{1,0:T(8,128)S(1)}, u32[]{:S(2)}, u32[]{:S(2)}) %collective-permute-start.7) | collective-permute-done | bytes 73760 | tf_op jit(solution)/shard_map/ppermute | solution.py:55
  25.0 0.3 send1.1
  25.3 1.2 %collective-permute-start.8 = (f32[144,128]{1,0:T(8,128)S(1)}, f32[144,128]{1,0:T(8,128)S(1)}, u32[]{:S(2)}, u32[]{:S(2)}) collective-permute-start(f32[144,128]{1,0:T(8,128)S(1)} %send1.1), channel_id=1, source_target_pairs={{0,4},{1,5},{2,6},{3,7},{4,0},{5,1},{6,2},{7,3},{8,12},{9,13},{10,... | collective-permute-start | bytes 221192 | tf_op jit(solution)/shard_map/ppermute | solution.py:55
  26.5 0.4 %edge1.1 = (f32[432,128]{1,0:T(8,128)S(1)}, f32[432,128]{1,0:T(8,128)S(1)}, f32[64,128]{1,0:T(8,128)S(1)}) custom-call(f32[144,128]{1,0:T(8,128)S(1)} %collective-permute-done.7.refs_0_, f32[1728,128]{1,0:T(8,128)S(1)} %get-tuple-element.70.refs_1_.early, f32[1728,128]{1,0:T(8,128)S(1)} %get-tuple-element.71.refs_2_.late, ...), custom_call_target="tpu_custom_call" | custom-call | flops 327680 | bytes 4972544 | tf_op jit(solution)/shard_map/edge1/pallas_call | solution.py:651
  26.9 1.6 %inner0.1 = (f32[1728,128]{1,0:T(8,128)}, f32[216,128]{1,0:T(8,128)S(1)}, f32[216,128]{1,0:T(8,128)S(1)}, f32[64,128]{1,0:T(8,128)S(1)}) custom-call(f32[1728,128]{1,0:T(8,128)S(1)} %get-tuple-element.70.refs_1_.early, f32[1728,128]{1,0:T(8,128)S(1)} %get-tuple-element.71.refs_2_.late, f32[512,128]{1,0:T(8,128)S(1)} %get-tuple-element.60.extra.refs_3_, ...), custom_call_target="tpu_custom_call" | custom-call | flops 3276800 | bytes 4956160 | tf_op jit(solution)/shard_map/inner0/pallas_call | solution.py:651
  28.5 1.3 %collective-permute-done.8.refs_0_ = f32[144,128]{1,0:T(8,128)S(1)} collective-permute-done((f32[144,128]{1,0:T(8,128)S(1)}, f32[144,128]{1,0:T(8,128)S(1)}, u32[]{:S(2)}, u32[]{:S(2)}) %collective-permute-start.8) | collective-permute-done | bytes 73760 | tf_op jit(solution)/shard_map/ppermute | solution.py:55
  29.7 1.4 %edge0.1 = (f32[216,8,128]{2,1,0:T(8,128)}, f32[64,128]{1,0:T(8,128)}) custom-call(f32[144,128]{1,0:T(8,128)S(1)} %collective-permute-done.8.refs_0_, f32[216,128]{1,0:T(8,128)S(1)} %get-tuple-element.78.refs_1_, f32[216,128]{1,0:T(8,128)S(1)} %get-tuple-element.79.refs_2_, ...), custom_call_target="tpu_custom_call", output_to_operand_aliasing={{0}: (9, {})} | custom-call | flops 327680 | bytes 3702784 | tf_op jit(solution)/shard_map/edge0/pallas_call | solution.py:651
  (2 shorter events, 0.0 us)
Async XLA Ops:
  3.0 11.0 %collective-permute-start.2 = (f32[520,128]{1,0:T(8,128)S(1)}, f32[520,128]{1,0:T(8,128)S(1)}, u32[]{:S(2)}, u32[]{:S(2)}) collective-permute-start(f32[520,128]{1,0:T(8,128)S(1)} %get-tuple-element.49), channel_id=1, source_target_pairs={{0,8},{1,9},{2,10},{3,11},{8,0},{9,1},{10,2},{11,3},{16,24},{17,25... | collective-permute-start | bytes 798728 | tf_op jit(solution)/shard_map/xswap/ppermute | solution.py:55
  6.1 7.9 %collective-permute-start.3 = (f32[520,128]{1,0:T(8,128)S(1)}, f32[520,128]{1,0:T(8,128)S(1)}, u32[]{:S(2)}, u32[]{:S(2)}) collective-permute-start(f32[520,128]{1,0:T(8,128)S(1)} %get-tuple-element.50), channel_id=1, source_target_pairs={{0,1},{1,0},{2,3},{3,2},{8,16},{9,17},{10,18},{11,19},{16,8},{17,9... | collective-permute-start | bytes 798728 | tf_op jit(solution)/shard_map/xswap/ppermute | solution.py:55
  6.1 1.6 %collective-permute-start = (f32[72,128]{1,0:T(8,128)S(1)}, f32[72,128]{1,0:T(8,128)S(1)}, u32[]{:S(2)}, u32[]{:S(2)}) collective-permute-start(f32[72,128]{1,0:T(8,128)S(1)} %get-tuple-element.44), channel_id=1, source_target_pairs={{0,1},{1,0},{2,3},{3,2},{4,5},{5,4},{6,7},{7,6},{8,9},{9,8},{10,11... | collective-permute-start | bytes 110600 | tf_op jit(solution)/shard_map/zswap/ppermute | solution.py:55
  6.6 3.6 %collective-permute-start.1 = (f32[72,128]{1,0:T(8,128)S(1)}, f32[72,128]{1,0:T(8,128)S(1)}, u32[]{:S(2)}, u32[]{:S(2)}) collective-permute-start(f32[72,128]{1,0:T(8,128)S(1)} %get-tuple-element.45), channel_id=1, source_target_pairs={{0,3},{1,2},{2,1},{3,0},{4,7},{5,6},{6,5},{7,4},{8,11},{9,10},{10,... | collective-permute-start | bytes 110600 | tf_op jit(solution)/shard_map/zswap/ppermute | solution.py:55
  10.5 4.5 %collective-permute-start.4 = (f32[56,128]{1,0:T(8,128)S(1)}, f32[56,128]{1,0:T(8,128)S(1)}, u32[]{:S(2)}, u32[]{:S(2)}) collective-permute-start(f32[56,128]{1,0:T(8,128)S(1)} %get-tuple-element.55), channel_id=1, source_target_pairs={{0,8},{1,9},{2,10},{3,11},{8,0},{9,1},{10,2},{11,3},{16,24},{17,25... | collective-permute-start | bytes 86024 | tf_op jit(solution)/shard_map/smallswap/ppermute | solution.py:55
  13.0 2.0 %collective-permute-start.5 = (f32[56,128]{1,0:T(8,128)S(1)}, f32[56,128]{1,0:T(8,128)S(1)}, u32[]{:S(2)}, u32[]{:S(2)}) collective-permute-start(f32[56,128]{1,0:T(8,128)S(1)} %get-tuple-element.56), channel_id=1, source_target_pairs={{0,1},{1,0},{2,3},{3,2},{8,16},{9,17},{10,18},{11,19},{16,8},{17,9... | collective-permute-start | bytes 86024 | tf_op jit(solution)/shard_map/smallswap/ppermute | solution.py:55
  15.5 4.8 %collective-permute-start.6 = (f32[144,128]{1,0:T(8,128)S(1)}, f32[144,128]{1,0:T(8,128)S(1)}, u32[]{:S(2)}, u32[]{:S(2)}) collective-permute-start(f32[144,128]{1,0:T(8,128)S(1)} %get-tuple-element.57), channel_id=1, source_target_pairs={{0,4},{1,5},{2,6},{3,7},{4,0},{5,1},{6,2},{7,3},{8,12},{9,13},{10,... | collective-permute-start | bytes 221192 | tf_op jit(solution)/shard_map/ppermute | solution.py:55
  20.6 4.4 %collective-permute-start.7 = (f32[144,128]{1,0:T(8,128)S(1)}, f32[144,128]{1,0:T(8,128)S(1)}, u32[]{:S(2)}, u32[]{:S(2)}) collective-permute-start(f32[144,128]{1,0:T(8,128)S(1)} %send2.1), channel_id=1, source_target_pairs={{0,4},{1,5},{2,6},{3,7},{4,0},{5,1},{6,2},{7,3},{8,12},{9,13},{10,... | collective-permute-start | bytes 221192 | tf_op jit(solution)/shard_map/ppermute | solution.py:55
  25.3 4.4 %collective-permute-start.8 = (f32[144,128]{1,0:T(8,128)S(1)}, f32[144,128]{1,0:T(8,128)S(1)}, u32[]{:S(2)}, u32[]{:S(2)}) collective-permute-start(f32[144,128]{1,0:T(8,128)S(1)} %send1.1), channel_id=1, source_target_pairs={{0,4},{1,5},{2,6},{3,7},{4,0},{5,1},{6,2},{7,3},{8,12},{9,13},{10,... | collective-permute-start | bytes 221192 | tf_op jit(solution)/shard_map/ppermute | solution.py:55
